TPU v7x, 32 devices: a whole 2x2x4 slice. The times are simulated.
32 devices in a mesh: outer: 4 (over x, core), inner: 8 (over z, y).
Axes of the slice: x: 2, y: 2, z: 4, core: 2. Of those that a mesh axis runs over, the one named last changes fastest.
Arguments:
- query_tiles: bfloat16 [4096, 768], P(('outer', 'inner')), may hold values from -7 to 7
- key_tiles: bfloat16 [4096, 768], P(('outer', 'inner')), may hold values from -6 to 6
- value_tiles: bfloat16 [4096, 768], P(('outer', 'inner')), may hold values from -6 to 6
- cotangent: bfloat16 [4096, 768], P(('outer', 'inner')), may hold values from -6 to 6
- row_lengths: int32 [128], P(('outer', 'inner')), may hold values from 1 to 32
Outputs:
- attended: bfloat16 [4096, 768], P(('outer', 'inner'))
- query_grad: bfloat16 [4096, 768], P(('outer', 'inner'))
- key_grad: bfloat16 [4096, 768], P(('outer', 'inner'))
- value_grad: bfloat16 [4096, 768], P(('outer', 'inner'))
All inputs are finite; a program needn't handle non-finite values.
Results may differ from a plain program's by a relative error of at most 0.0203.
Values may be sent and summed in bfloat16 or wider, within the bound.
A program may use at most 128 MiB of HBM per device.

v0:
```python
import jax
import jax.numpy as jnp
import numpy as np
from jax import lax
from jax.sharding import PartitionSpec as P

HEADS = 16
HEAD = 48
ROW = 32
STRIDE_GROUP = 4
STRIDE_SLIDE = 16


NEGATIVE_FILL = -1e30
heads_at_once = 4


def as_sent(value):

    def short(part):
        return part.astype(jnp.bfloat16) if part.dtype == jnp.float32 else part

    return jax.tree.map(short, value)


def head_ranges(head_total):
    step_size = min(head_total, heads_at_once)
    return [(first_head, first_head + step_size) for first_head in range(0, head_total, step_size)]


def scores_of(query_block, key_block, score_scale):
    return (
        jnp.einsum("hdq,hdk->hqk", query_block, key_block, preferred_element_type=jnp.float32)
        * score_scale
    )


def branch_stats(query_heads, key_heads, value_heads, key_valid, score_scale):
    peak_list, total_list, sum_list = ([], [], [])
    for first_head, last_head in head_ranges(query_heads.shape[0]):
        raw_scores = scores_of(
            query_heads[first_head:last_head], key_heads[first_head:last_head], score_scale
        )
        key_keep = key_valid[first_head:last_head][:, None, :]
        masked = jnp.where(key_keep, raw_scores, NEGATIVE_FILL)
        row_peak = jnp.max(masked, axis=2)
        weights = jnp.where(key_keep, jnp.exp(masked - row_peak[:, :, None]), 0.0)
        peak_list.append(row_peak)
        total_list.append(jnp.sum(weights, axis=2))
        sum_list.append(
            jnp.einsum(
                "hqk,hdk->hdq",
                weights.astype(jnp.bfloat16),
                value_heads[first_head:last_head],
                preferred_element_type=jnp.float32,
            )
        )
    return (
        jnp.concatenate(peak_list, axis=0),
        jnp.concatenate(total_list, axis=0),
        jnp.concatenate(sum_list, axis=0),
    )


def branch_grads(
    query_heads,
    key_heads,
    value_heads,
    cotan_heads,
    log_norm,
    out_dot,
    key_valid,
    score_scale,
    want_query,
    want_keys,
):
    query_list, key_list, value_list = ([], [], [])
    for first_head, last_head in head_ranges(query_heads.shape[0]):
        query_block = query_heads[first_head:last_head]
        key_block = key_heads[first_head:last_head]
        cotan_block = cotan_heads[first_head:last_head]
        raw_scores = scores_of(query_block, key_block, score_scale)
        key_keep = key_valid[first_head:last_head][:, None, :]
        weights = jnp.where(
            key_keep, jnp.exp(raw_scores - log_norm[first_head:last_head][:, :, None]), 0.0
        )
        weight_grads = jnp.einsum(
            "hdq,hdk->hqk",
            cotan_block,
            value_heads[first_head:last_head],
            preferred_element_type=jnp.float32,
        )
        low_grads = (weights * (weight_grads - out_dot[first_head:last_head][:, :, None])).astype(
            jnp.bfloat16
        )
        if want_query:
            query_list.append(
                score_scale
                * jnp.einsum(
                    "hqk,hdk->hdq", low_grads, key_block, preferred_element_type=jnp.float32
                )
            )
        if want_keys:
            key_list.append(
                score_scale
                * jnp.einsum(
                    "hqk,hdq->hdk", low_grads, query_block, preferred_element_type=jnp.float32
                )
            )
            value_list.append(
                jnp.einsum(
                    "hqk,hdq->hdk",
                    weights.astype(jnp.bfloat16),
                    cotan_block,
                    preferred_element_type=jnp.float32,
                )
            )
    query_part = jnp.concatenate(query_list, axis=0) if want_query else None
    key_part = jnp.concatenate(key_list, axis=0) if want_keys else None
    value_part = jnp.concatenate(value_list, axis=0) if want_keys else None
    return (query_part, key_part, value_part)


def head_offsets(head_total, stride):
    return np.arange(head_total) * stride // head_total


def select_rows(array_in, stride):
    head_total = array_in.shape[0]
    offsets = head_offsets(head_total, stride)
    folded = array_in.reshape(array_in.shape[:-1] + (array_in.shape[-1] // stride, stride))
    return jnp.stack(
        [folded[head_index, ..., int(offsets[head_index])] for head_index in range(head_total)]
    )


def spread_rows(array_in, stride, fill_value):
    head_total = array_in.shape[0]
    chosen = np.arange(stride)[None, :] == head_offsets(head_total, stride)[:, None]
    chosen = chosen.reshape((head_total,) + (1,) * (array_in.ndim - 1) + (stride,))
    full = jnp.where(chosen, array_in[..., None], fill_value)
    return full.reshape(array_in.shape[:-1] + (array_in.shape[-1] * stride,))


def to_heads(flat_in):
    return jnp.transpose(flat_in.reshape(flat_in.shape[0], HEADS, -1), (1, 2, 0))


def to_flat(heads_in):
    return jnp.transpose(heads_in, (2, 0, 1)).reshape(heads_in.shape[2], -1)


def local(query_tiles, key_tiles, value_tiles, cotangent, row_lengths):
    tile_count = query_tiles.shape[0]
    score_scale = HEAD ** (-0.5)
    query_heads = to_heads(query_tiles)
    key_heads = to_heads(key_tiles)
    value_heads = to_heads(value_tiles)
    cotan_heads = to_heads(cotangent)
    tile_slot = jnp.arange(tile_count, dtype=jnp.int32)
    tile_valid = tile_slot % ROW < jnp.repeat(row_lengths, ROW, total_repeat_length=tile_count)
    valid_heads = jnp.broadcast_to(tile_valid[None, :], (HEADS, tile_count))
    group_query = select_rows(query_heads, STRIDE_GROUP)
    group_key = select_rows(key_heads, STRIDE_GROUP)
    group_value = select_rows(value_heads, STRIDE_GROUP)
    group_cotan = select_rows(cotan_heads, STRIDE_GROUP)
    group_valid = select_rows(valid_heads, STRIDE_GROUP)
    group_flag = group_valid.astype(jnp.bfloat16)[:, None, :]
    slide_query = select_rows(query_heads, STRIDE_SLIDE)
    slide_key = select_rows(key_heads, STRIDE_SLIDE)
    slide_value = select_rows(value_heads, STRIDE_SLIDE)
    slide_flag = select_rows(valid_heads, STRIDE_SLIDE).astype(jnp.bfloat16)[:, None, :]
    owned_query, owned_key, owned_value, owned_flag = (
        lax.all_to_all(slide_query, "outer", split_axis=0, concat_axis=2, tiled=True),
        lax.all_to_all(slide_key, "outer", split_axis=0, concat_axis=2, tiled=True),
        lax.all_to_all(slide_value, "outer", split_axis=0, concat_axis=2, tiled=True),
        lax.all_to_all(slide_flag, "outer", split_axis=0, concat_axis=2, tiled=True),
    )
    got_group = (
        lax.all_gather(group_key, "inner", axis=2, tiled=True),
        lax.all_gather(group_value, "inner", axis=2, tiled=True),
        lax.all_gather(group_flag, "inner", axis=2, tiled=True),
    )
    got_slide = (
        lax.all_gather(owned_key, "inner", axis=2, tiled=True),
        lax.all_gather(owned_value, "inner", axis=2, tiled=True),
        lax.all_gather(owned_flag, "inner", axis=2, tiled=True),
    )
    near_peak, near_total, near_sum = branch_stats(
        query_heads, key_heads, value_heads, valid_heads, score_scale
    )
    remote_group_key = got_group[0]
    remote_group_value = got_group[1]
    remote_group_valid = got_group[2][:, 0, :] > 0.5
    group_peak, group_total, group_sum = branch_stats(
        group_query, remote_group_key, remote_group_value, remote_group_valid, score_scale
    )
    slide_all_key = got_slide[0]
    slide_all_value = got_slide[1]
    slide_all_valid = got_slide[2][:, 0, :] > 0.5
    owner_peak, owner_total, owner_sum = branch_stats(
        owned_query, slide_all_key, slide_all_value, slide_all_valid, score_scale
    )
    slide_peak, slide_total, slide_sum = (
        lax.all_to_all(owner_peak[:, None, :], "outer", split_axis=2, concat_axis=0, tiled=True),
        lax.all_to_all(owner_total[:, None, :], "outer", split_axis=2, concat_axis=0, tiled=True),
        lax.all_to_all(owner_sum, "outer", split_axis=2, concat_axis=0, tiled=True),
    )
    slide_peak = slide_peak[:, 0, :]
    slide_total = slide_total[:, 0, :]
    group_peak_full = spread_rows(group_peak, STRIDE_GROUP, NEGATIVE_FILL)
    slide_peak_full = spread_rows(slide_peak, STRIDE_SLIDE, NEGATIVE_FILL)
    best_peak = jnp.maximum(jnp.maximum(near_peak, group_peak_full), slide_peak_full)
    near_weight = jnp.exp(near_peak - best_peak)
    group_weight = jnp.exp(group_peak_full - best_peak)
    slide_weight = jnp.exp(slide_peak_full - best_peak)
    denominator = (
        near_total * near_weight
        + spread_rows(group_total, STRIDE_GROUP, 0.0) * group_weight
        + spread_rows(slide_total, STRIDE_SLIDE, 0.0) * slide_weight
    )
    numerator = (
        near_sum * near_weight[:, None, :]
        + spread_rows(group_sum, STRIDE_GROUP, 0.0) * group_weight[:, None, :]
        + spread_rows(slide_sum, STRIDE_SLIDE, 0.0) * slide_weight[:, None, :]
    )
    attended = (numerator / denominator[:, None, :]).astype(jnp.bfloat16)
    log_norm = best_peak + jnp.log(denominator)
    out_dot = jnp.sum(cotan_heads.astype(jnp.float32) * attended.astype(jnp.float32), axis=1)
    near_query, near_key, near_value = branch_grads(
        query_heads,
        key_heads,
        value_heads,
        cotan_heads,
        log_norm,
        out_dot,
        valid_heads,
        score_scale,
        True,
        True,
    )
    group_lse = select_rows(log_norm, STRIDE_GROUP)
    group_dot = select_rows(out_dot, STRIDE_GROUP)
    group_query_grad = branch_grads(
        group_query,
        remote_group_key,
        remote_group_value,
        group_cotan,
        group_lse,
        group_dot,
        remote_group_valid,
        score_scale,
        True,
        False,
    )[0]
    got_group_rows = (
        lax.all_gather(group_query, "inner", axis=2, tiled=True),
        lax.all_gather(group_cotan, "inner", axis=2, tiled=True),
    )
    got_group_stats = (
        lax.all_gather(group_lse, "inner", axis=1, tiled=True),
        lax.all_gather(group_dot, "inner", axis=1, tiled=True),
    )
    unused_group, group_key_grad, group_value_grad = branch_grads(
        got_group_rows[0],
        group_key,
        group_value,
        got_group_rows[1],
        got_group_stats[0],
        got_group_stats[1],
        group_valid,
        score_scale,
        False,
        True,
    )
    slide_cotan = select_rows(cotan_heads, STRIDE_SLIDE)
    slide_lse = select_rows(log_norm, STRIDE_SLIDE)
    slide_dot = select_rows(out_dot, STRIDE_SLIDE)
    owned_cotan = lax.all_to_all(slide_cotan, "outer", split_axis=0, concat_axis=2, tiled=True)
    owned_lse, owned_dot = (
        lax.all_to_all(slide_lse, "outer", split_axis=0, concat_axis=1, tiled=True),
        lax.all_to_all(slide_dot, "outer", split_axis=0, concat_axis=1, tiled=True),
    )
    owned_query_grad, partial_key, partial_value = branch_grads(
        owned_query,
        slide_all_key,
        slide_all_value,
        owned_cotan,
        owned_lse,
        owned_dot,
        slide_all_valid,
        score_scale,
        True,
        True,
    )
    owned_key_grad, owned_value_grad = (
        lax.psum_scatter(
            partial_key.astype(jnp.bfloat16), "inner", scatter_dimension=2, tiled=True
        ).astype(jnp.float32),
        lax.psum_scatter(
            partial_value.astype(jnp.bfloat16), "inner", scatter_dimension=2, tiled=True
        ).astype(jnp.float32),
    )
    slide_query_grad, slide_key_grad, slide_value_grad = (
        lax.all_to_all(
            as_sent(owned_query_grad), "outer", split_axis=2, concat_axis=0, tiled=True
        ).astype(owned_query_grad.dtype),
        lax.all_to_all(
            owned_key_grad.astype(jnp.bfloat16), "outer", split_axis=2, concat_axis=0, tiled=True
        ).astype(owned_key_grad.dtype),
        lax.all_to_all(
            owned_value_grad.astype(jnp.bfloat16), "outer", split_axis=2, concat_axis=0, tiled=True
        ).astype(owned_value_grad.dtype),
    )
    query_grad = (
        near_query
        + spread_rows(group_query_grad, STRIDE_GROUP, 0.0)
        + spread_rows(slide_query_grad, STRIDE_SLIDE, 0.0)
    )
    key_grad = (
        near_key
        + spread_rows(group_key_grad, STRIDE_GROUP, 0.0)
        + spread_rows(slide_key_grad, STRIDE_SLIDE, 0.0)
    )
    value_grad = (
        near_value
        + spread_rows(group_value_grad, STRIDE_GROUP, 0.0)
        + spread_rows(slide_value_grad, STRIDE_SLIDE, 0.0)
    )
    return (
        to_flat(attended),
        to_flat(query_grad.astype(jnp.bfloat16)),
        to_flat(key_grad.astype(jnp.bfloat16)),
        to_flat(value_grad.astype(jnp.bfloat16)),
    )


def solution(mesh):
    in_specs = (
        P(("outer", "inner"), None),
        P(("outer", "inner"), None),
        P(("outer", "inner"), None),
        P(("outer", "inner"), None),
        P(("outer", "inner")),
    )
    out_specs = (
        P(("outer", "inner"), None),
        P(("outer", "inner"), None),
        P(("outer", "inner"), None),
        P(("outer", "inner"), None),
    )
    return jax.shard_map(local, mesh=mesh, in_specs=in_specs, out_specs=out_specs, check_vma=False)
```

profile of v0, /device:TPU:0, one launch (start us, length us, event | category | flops | bytes accessed | tf_op | source)
XLA Modules:
  0.0 621.1 jit_solution(8717144641494858951)
XLA Ops:
  13.2 4.2 all-to-all-start
  45.8 34.4 %all_gather.31 = bf16[16,48,256]{1,0,2:T(8,128)(2,1)S(1)} all-gather(bf16[16,48,32]{1,0,2:T(8,128)(2,1)S(1)} %copy.4734), channel_id=1, replica_groups=mesh['outer'=4,'inner'=8] {'inner'}, dimensions={2}, use_global_device_ids=true | all-gather | bytes 442368 | tf_op jit(solution)/shard_map/all_gather | solution.py:180
  83.1 30.5 %all_gather.30 = bf16[16,1,256]{0,1,2:T(2,128)(2,1)S(1)} all-gather(bf16[16,1,32]{0,1,2:T(2,128)(2,1)S(1)} %copy.4710), channel_id=1, replica_groups=mesh['outer'=4,'inner'=8] {'inner'}, dimensions={2}, use_global_device_ids=true | all-gather | bytes 9216 | tf_op jit(solution)/shard_map/all_gather | solution.py:182
  127.5 33.5 %all_gather.34 = bf16[16,48,256]{1,0,2:T(8,128)(2,1)S(1)} all-gather(bf16[16,48,32]{1,0,2:T(8,128)(2,1)S(1)} %copy.4785), channel_id=1, replica_groups=mesh['outer'=4,'inner'=8] {'inner'}, dimensions={2}, use_global_device_ids=true | all-gather | bytes 442368 | tf_op jit(solution)/shard_map/all_gather | solution.py:181
  183.1 33.4 %all_gather.36 = bf16[16,48,256]{1,2,0:T(8,128)(2,1)S(1)} all-gather(bf16[16,48,32]{1,2,0:T(8,128)(2,1)S(1)} %get-tuple-element.227), channel_id=1, replica_groups=mesh['outer'=4,'inner'=8] {'inner'}, dimensions={2}, use_global_device_ids=true | all-gather | bytes 442368 | tf_op jit(solution)/shard_map/all_gather | solution.py:257
  226.4 32.0 %all_gather.38 = bf16[16,48,256]{1,2,0:T(8,128)(2,1)S(1)} all-gather(bf16[16,48,32]{1,2,0:T(8,128)(2,1)S(1)} %get-tuple-element.195), channel_id=1, replica_groups=mesh['outer'=4,'inner'=8] {'inner'}, dimensions={2}, use_global_device_ids=true | all-gather | bytes 442368 | tf_op jit(solution)/shard_map/all_gather | solution.py:258
  266.9 3.7 all-to-all-start.2
  285.3 30.5 %all_gather.32 = bf16[4,1,256]{0,1,2:T(2,128)(2,1)S(1)} all-gather(bf16[4,1,32]{0,1,2:T(2,128)(2,1)S(1)} %copy.4757), channel_id=1, replica_groups=mesh['outer'=4,'inner'=8] {'inner'}, dimensions={2}, use_global_device_ids=true | all-gather | bytes 2304 | tf_op jit(solution)/shard_map/all_gather | solution.py:187
  316.0 3.4 all-to-all-start.4
  319.5 3.7 all-to-all-done.4
  326.4 30.8 %all_gather.33 = bf16[4,48,256]{1,2,0:T(8,128)(2,1)S(1)} all-gather(bf16[4,48,32]{1,2,0:T(8,128)(2,1)S(1)} %bitcast.763), channel_id=1, replica_groups=mesh['outer'=4,'inner'=8] {'inner'}, dimensions={2}, use_global_device_ids=true | all-gather | bytes 110592 | tf_op jit(solution)/shard_map/all_gather | solution.py:185
  357.3 3.3 all-to-all-start.8
  361.4 31.0 %all_gather.35 = bf16[4,48,256]{1,2,0:T(8,128)(2,1)S(1)} all-gather(bf16[4,48,32]{1,2,0:T(8,128)(2,1)S(1)} %bitcast.761), channel_id=1, replica_groups=mesh['outer'=4,'inner'=8] {'inner'}, dimensions={2}, use_global_device_ids=true | all-gather | bytes 110592 | tf_op jit(solution)/shard_map/all_gather | solution.py:186
  393.1 3.2 all-to-all-start.6
  400.2 3.2 all-to-all-start.3
  413.7 30.5 %all-gather = f32[8,32,16]{1,2,0:T(8,128)S(1)} all-gather(f32[1,32,16]{1,2,0:T(8,128)S(1)} %bitcast.789), channel_id=1, replica_groups=mesh['outer'=4,'inner'=8] {'inner'}, dimensions={0}, use_global_device_ids=true | all-gather | bytes 18432 | tf_op jit(solution)/shard_map/all_gather | solution.py:261
  446.0 4.1 all-to-all-start.7
  463.3 3.4 all-to-all-start.5
  485.7 30.5 %all-gather.1 = f32[8,32,16]{1,2,0:T(8,128)S(1)} all-gather(f32[1,32,16]{1,2,0:T(8,128)S(1)} %bitcast.788), channel_id=1, replica_groups=mesh['outer'=4,'inner'=8] {'inner'}, dimensions={0}, use_global_device_ids=true | all-gather | bytes 18432 | tf_op jit(solution)/shard_map/all_gather | solution.py:262
  523.3 3.4 all-to-all-start.9
  534.2 3.3 all-to-all-start.10
  542.9 3.3 all-to-all-start.12
  546.6 3.4 all-to-all-done.12
  550.5 53.0 %reduce-scatter.3.cloned.1.call-done = bf16[4,48,32]{1,2,0:T(8,128)(2,1)} async-done(((bf16[4,48,256]{1,2,0:T(8,128)(2,1)}), bf16[4,48,32]{1,2,0:T(8,128)(2,1)}) %reduce-scatter.3.cloned.1.call-update) | async-done | bytes 12304 | tf_op jit(solution)/shard_map/reduce_scatter | solution.py:297
  (883 shorter events, 188.7 us)
Async XLA Ops:
  11.9 22.3 %copy-start.161 = (pred[128]{0:T(512)(128)(4,1)}, pred[128]{0:T(512)(128)(4,1)S(1)}, u32[]{:S(2)}) copy-start(pred[128]{0:T(512)(128)(4,1)S(1)} %get-tuple-element.266) | copy-start | bytes 388
  13.2 253.7 %all-to-all-start = ((bf16[16,1,8]{2,1,0:T(2,128)(2,1)}), bf16[16,1,8]{2,1,0:T(2,128)(2,1)}, u32[]{:S(2)}, u32[]{:S(2)}) async-start(bf16[16,1,8]{2,1,0:T(2,128)(2,1)} %convert_element_type.197), calls=%async_computation | async-start | bytes 16384 | tf_op jit(solution)/shard_map/all_to_all | solution.py:177
  21.9 12.3 %copy-start.14 = (bf16[128,768]{0,1:T(8,128)(2,1)}, bf16[128,768]{0,1:T(8,128)(2,1)S(1)}, u32[]{:S(2)}) copy-start(bf16[128,768]{0,1:T(8,128)(2,1)S(1)} %copy.4705) | copy-start | bytes 589828
  24.1 10.1 %copy-start.41 = (f32[4,128,128]{1,2,0:T(8,128)}, f32[4,128,128]{1,2,0:T(8,128)S(1)}, u32[]{:S(2)}) copy-start(f32[4,128,128]{1,2,0:T(8,128)S(1)} %get-tuple-element.501) | copy-start | bytes 786436
  24.1 10.1 %copy-start.157 = (f32[4,128]{1,0:T(4,128)}, f32[4,128]{1,0:T(4,128)S(1)}, u32[]{:S(2)}) copy-start(f32[4,128]{1,0:T(4,128)S(1)} %get-tuple-element.500) | copy-start | bytes 6148
  266.9 49.0 %all-to-all-start.2 = ((bf16[4,2,768]{2,1,0:T(2,128)(2,1)}), bf16[4,2,768]{2,1,0:T(2,128)(2,1)S(1)}, u32[]{:S(2)}, u32[]{:S(2)}) async-start(bf16[4,2,768]{2,1,0:T(2,128)(2,1)} %reshape.1194), calls=%async_computation.2 | async-start | bytes 24576 | tf_op jit(solution)/shard_map/all_to_all | solution.py:175
  316.0 7.2 %all-to-all-start.4 = ((bf16[4,2,768]{2,1,0:T(2,128)(2,1)}), bf16[4,2,768]{2,1,0:T(2,128)(2,1)S(1)}, u32[]{:S(2)}, u32[]{:S(2)}) async-start(bf16[4,2,768]{2,1,0:T(2,128)(2,1)} %reshape.1192), calls=%async_computation.4 | async-start | bytes 24576 | tf_op jit(solution)/shard_map/all_to_all | solution.py:176
  319.3 77.0 %copy-start.107 = (pred[4,256]{1,0:T(4,128)(4,1)}, pred[4,256]{1,0:T(4,128)(4,1)S(1)}, u32[]{:S(2)}) copy-start(pred[4,256]{1,0:T(4,128)(4,1)S(1)} %compare_bitcast_fusion) | copy-start | bytes 3076
  323.2 34.1 %all-to-all-start.1 = ((bf16[4,2,768]{2,1,0:T(2,128)(2,1)}), bf16[4,2,768]{2,1,0:T(2,128)(2,1)S(1)}, u32[]{:S(2)}, u32[]{:S(2)}) async-start(bf16[4,2,768]{2,1,0:T(2,128)(2,1)} %reshape.1196), calls=%async_computation.1 | async-start | bytes 24576 | tf_op jit(solution)/shard_map/all_to_all | solution.py:174
  357.3 35.8 %all-to-all-start.8 = ((bf16[4,2,768]{2,1,0:T(2,128)(2,1)}), bf16[4,2,768]{2,1,0:T(2,128)(2,1)S(1)}, u32[]{:S(2)}, u32[]{:S(2)}) async-start(bf16[4,2,768]{2,1,0:T(2,128)(2,1)} %reshape.1200), calls=%async_computation.8 | async-start | bytes 24576 | tf_op jit(solution)/shard_map/all_to_all | solution.py:279
  361.2 35.1 %copy-start.2 = (f32[4,32,256]{2,1,0:T(8,128)}, f32[4,32,256]{2,1,0:T(8,128)S(1)}, u32[]{:S(2)}) copy-start(f32[4,32,256]{2,1,0:T(8,128)S(1)} %get-tuple-element.504) | copy-start | bytes 393220
  393.1 7.1 %all-to-all-start.6 = ((f32[4,1,32]{0,1,2:T(1,128)}), f32[4,1,32]{0,1,2:T(1,128)S(1)}, u32[]{:S(2)}, u32[]{:S(2)}) async-start(f32[4,1,32]{0,1,2:T(1,128)} %copy.4801), calls=%async_computation.6 | async-start | bytes 32768 | tf_op jit(solution)/shard_map/all_to_all | solution.py:206
  396.6 11.5 %copy-start.31 = (f32[16,32,4]{2,1,0:T(8,128)S(1)}, f32[16,32,4]{2,1,0:T(8,128)}, u32[]{:S(2)}) copy-start(f32[16,32,4]{2,1,0:T(8,128)} %copy-done.30) | copy-start | bytes 24580
  400.2 7.1 %all-to-all-start.3 = ((f32[4,1,32]{0,1,2:T(1,128)}), f32[4,1,32]{0,1,2:T(1,128)S(1)}, u32[]{:S(2)}, u32[]{:S(2)}) async-start(f32[4,1,32]{0,1,2:T(1,128)} %copy.4763), calls=%async_computation.3 | async-start | bytes 32768 | tf_op jit(solution)/shard_map/all_to_all | solution.py:205
  446.0 17.2 %all-to-all-start.7 = ((f32[4,4,8]{2,1,0:T(4,128)}), f32[4,4,8]{2,1,0:T(4,128)}, u32[]{:S(2)}, u32[]{:S(2)}) async-start(f32[4,4,8]{2,1,0:T(4,128)} %bitcast.135), calls=%async_computation.7 | async-start | bytes 16384 | tf_op jit(solution)/shard_map/all_to_all | solution.py:281
  463.3 7.3 %all-to-all-start.5 = ((f32[4,1,1536]{2,1,0:T(1,128)}), f32[4,1,1536]{2,1,0:T(1,128)S(1)}, u32[]{:S(2)}, u32[]{:S(2)}) async-start(f32[4,1,1536]{2,1,0:T(1,128)} %reshape.1198), calls=%async_computation.5 | async-start | bytes 49152 | tf_op jit(solution)/shard_map/all_to_all | solution.py:207
  466.7 74.8 %reduce-scatter.5.cloned.1.call-start = ((), (), s32[]{:S(2)}) async-start(), calls=%async_computation.16 | async-start | bytes 294912 | tf_op jit(solution)/shard_map/reduce_scatter | solution.py:300
  523.3 9.0 %all-to-all-start.9 = ((f32[4,4,8]{2,1,0:T(4,128)}), f32[4,4,8]{2,1,0:T(4,128)S(1)}, u32[]{:S(2)}, u32[]{:S(2)}) async-start(f32[4,4,8]{2,1,0:T(4,128)} %bitcast.141), calls=%async_computation.9 | async-start | bytes 16384 | tf_op jit(solution)/shard_map/all_to_all | solution.py:282
  534.2 7.1 %all-to-all-start.10 = ((bf16[4,2,768]{2,1,0:T(2,128)(2,1)}), bf16[4,2,768]{2,1,0:T(2,128)(2,1)S(1)}, u32[]{:S(2)}, u32[]{:S(2)}) async-start(bf16[4,2,768]{2,1,0:T(2,128)(2,1)} %reshape.1202), calls=%async_computation.10 | async-start | bytes 24576 | tf_op jit(solution)/shard_map/all_to_all | solution.py:305
  537.5 66.1 %reduce-scatter.3.cloned.1.call-start = ((), (), s32[]{:S(2)}) async-start(), calls=%async_computation.15 | async-start | bytes 294912 | tf_op jit(solution)/shard_map/reduce_scatter | solution.py:297
  542.9 7.1 %all-to-all-start.12 = ((bf16[4,2,768]{2,1,0:T(2,128)(2,1)}), bf16[4,2,768]{2,1,0:T(2,128)(2,1)S(1)}, u32[]{:S(2)}, u32[]{:S(2)}) async-start(bf16[4,2,768]{2,1,0:T(2,128)(2,1)} %reshape.1206), calls=%async_computation.14 | async-start | bytes 24576 | tf_op jit(solution)/shard_map/all_to_all | solution.py:311
  550.2 58.1 %copy-start.16 = (f32[16,48,128]{2,1,0:T(8,128)S(1)}, f32[16,48,128]{2,1,0:T(8,128)}, u32[]{:S(2)}) copy-start(f32[16,48,128]{2,1,0:T(8,128)} %copy.4886) | copy-start | bytes 1179652
  550.5 57.7 %copy-start.32 = (f32[4,48,128]{2,1,0:T(8,128)S(1)}, f32[4,48,128]{2,1,0:T(8,128)}, u32[]{:S(2)}) copy-start(f32[4,48,128]{2,1,0:T(8,128)} %fusion.40) | copy-start | bytes 294916
  605.0 7.0 %all-to-all-start.11 = ((bf16[4,2,768]{2,1,0:T(2,128)(2,1)}), bf16[4,2,768]{2,1,0:T(2,128)(2,1)S(1)}, u32[]{:S(2)}, u32[]{:S(2)}) async-start(bf16[4,2,768]{2,1,0:T(2,128)(2,1)} %reshape.1204), calls=%async_computation.12 | async-start | bytes 24576 | tf_op jit(solution)/shard_map/all_to_all | solution.py:308
  (210 other events, 376.9 us)
Sparse Core Ops, SparseCore 0:
  470.8 62.0 reduce-scatter.4
  541.6 61.8 reduce-scatter.2
where the time goes:
time: 625 us; the launch traced here: 621 us
  blocking collectives  317 us (51%)
  local copies, waits for them, and re-layouts  133 us (21%)
  waiting for transfers between devices  68.5 us (11%)
  starting transfers between devices  44.9 us (7%)
  matrix products  25.8 us (4%)
  between operations  16.8 us (3%)
  other arithmetic  14.8 us (2%)
    unnamed x631, local copies, waits for them, and re-layouts  80.9 us
    reduce_scatter x1, waiting for transfers between devices, local(): lax.psum_scatter(partial_key.astype(jnp.bfloat16), 'inner', scatter_dimen...  53 us
    all_gather x1, blocking collectives, local(): lax.all_gather(group_key, 'inner', axis=2, tiled=True)  34.4 us
    all_gather x1, blocking collectives, local(): lax.all_gather(group_value, 'inner', axis=2, tiled=True)  33.5 us
    all_gather x1, blocking collectives, local(): lax.all_gather(group_query, 'inner', axis=2, tiled=True)  33.4 us
    all_gather x1, blocking collectives, local(): lax.all_gather(group_cotan, 'inner', axis=2, tiled=True)  32 us
    all_gather x1, blocking collectives, local(): lax.all_gather(owned_value, 'inner', axis=2, tiled=True)  31 us
    all_gather x1, blocking collectives, local(): lax.all_gather(owned_key, 'inner', axis=2, tiled=True)  30.8 us
  transfers between devices with their start and end apart: 15, of which 8 were waited for; matrix products, arithmetic and copies ran while one was open for 20% of the time, Pallas kernels for 0%

commit v1 on v0

--- a/solution.py
+++ b/solution.py
@@ -2,6 +2,8 @@
 import jax.numpy as jnp
 import numpy as np
 from jax import lax
+from jax.experimental import pallas as pl
+from jax.experimental.pallas import tpu as pltpu
 from jax.sharding import PartitionSpec as P
 
 HEADS = 16
@@ -335,18 +337,414 @@
     )
 
 
+BF = jnp.bfloat16
+F32 = jnp.float32
+LANES = 128
+SCALE = HEAD ** (-0.5)
+PAIR = 2 * HEAD
+
+
+def window(first_col, width):
+    start = first_col // LANES * LANES
+    shift = first_col - start
+    return start, (LANES if shift + width <= LANES else 2 * LANES), shift
+
+
+def iota2(shape, axis):
+    return lax.broadcasted_iota(jnp.int32, shape, axis)
+
+
+def original_tile(j):
+    return (j & 7) * 16 + ((j >> 3) & 3) * 4 + (j >> 5)
+
+
+def permute_matrix(inverse):
+    shape = (LANES, LANES)
+    j, i = (iota2(shape, 1), iota2(shape, 0)) if inverse else (iota2(shape, 0), iota2(shape, 1))
+    return (original_tile(j) == i).astype(F32).astype(BF)
+
+
+def key_bias(len_ref, axis):
+    tile = original_tile(iota2((LANES, LANES), axis))
+    row = tile >> 5
+    length = jnp.full((LANES, LANES), len_ref[0], jnp.int32)
+    for index in range(1, 4):
+        length = jnp.where(row == index, len_ref[index], length)
+    return jnp.where((tile & 31) < length, 0.0, NEGATIVE_FILL).astype(F32)
+
+
+def shift_in(width, shift, kept):
+    row, col = iota2((width, LANES), 0), iota2((width, LANES), 1)
+    return ((row - shift == col) & (col < kept)).astype(F32).astype(BF)
+
+
+def shift_out(width, shift, kept):
+    row, col = iota2((LANES, width), 0), iota2((LANES, width), 1)
+    return ((col - shift == row) & (row < kept)).astype(F32).astype(BF)
+
+
+def lane_mask(width, first, last, extra=-1):
+    lane = iota2((1, width), 1)
+    keep = (lane >= first) & (lane < last)
+    if extra >= 0:
+        keep = keep | (lane == extra)
+    return keep.astype(F32).astype(BF)
+
+
+def mm(a, b):
+    return jnp.dot(a, b, preferred_element_type=F32)
+
+
+def mm_t(a, b):
+    return lax.dot_general(a, b, (((1,), (1,)), ((), ())), preferred_element_type=F32)
+
+
+def t_mm(a, b):
+    return lax.dot_general(a, b, (((0,), (0,)), ((), ())), preferred_element_type=F32)
+
+
+def slide_row(r):
+    return (r % 4) * 32 + (r // 4) * 8
+
+
+def split_mm(a, onehot):
+    high = a.astype(BF)
+    low = (a - high.astype(F32)).astype(BF)
+    return mm(high, onehot) + mm(low, onehot)
+
+
+def prep_kernel(copies, len_ref, q_ref, k_ref, v_ref, c_ref, xp_ref, gs_ref, ss_ref):
+    perm = permute_matrix(False)
+    xs = []
+    for index, ref in enumerate((q_ref, k_ref, v_ref, c_ref)):
+        xs.append(mm(perm, ref[...]))
+        xp_ref[index] = xs[-1].astype(BF)
+    bias = key_bias(len_ref, 0)
+    for p in range(HEADS // 2):
+        row = p // 2 * 32
+        start, width, shift = window(PAIR * p, PAIR)
+        stacked = jnp.concatenate(
+            [x[row : row + 32, start : start + width].astype(BF) for x in xs], axis=0
+        )
+        moved = mm(stacked, shift_in(width, shift, PAIR))
+        flag = iota2((32, LANES), 1) == PAIR
+        gs_ref[p, 0] = jnp.where(flag, 1.0, moved[0:32]).astype(BF)
+        gs_ref[p, 1] = jnp.where(flag, bias[row : row + 32], moved[32:64]).astype(BF)
+        gs_ref[p, 2] = moved[64:96].astype(BF)
+        gs_ref[p, 3] = moved[96:128].astype(BF)
+    for r in range(HEADS):
+        row = slide_row(r)
+        start, width, shift = window(HEAD * r, HEAD)
+        stacked = jnp.concatenate(
+            [x[row : row + 8, start : start + width] for x in xs], axis=0
+        ).astype(BF)
+        moved = mm(stacked, shift_in(width, shift, HEAD))
+        flag = iota2((8, LANES), 1) == HEAD
+        block = jnp.concatenate(
+            [
+                jnp.where(flag, 1.0, moved[0:8]),
+                jnp.where(flag, bias[row : row + 8], moved[8:16]),
+                moved[16:32],
+            ],
+            axis=0,
+        ).astype(BF)
+        for copy in range(copies):
+            ss_ref[copy * HEADS + r] = block
+
+
+def near_fwd_kernel(len_ref, xp_ref, o_ref, lse_ref):
+    bias = key_bias(len_ref, 1)
+    lane = iota2((LANES, LANES), 1)
+    lse = jnp.full((LANES, LANES), NEGATIVE_FILL, F32)
+    total = [None] * (HEADS * HEAD // LANES)
+    for h in range(HEADS):
+        start, width, shift = window(HEAD * h, HEAD)
+        mask = lane_mask(width, shift, shift + HEAD)
+        s = mm_t(xp_ref[0, :, start : start + width] * mask, xp_ref[1, :, start : start + width])
+        s = s * SCALE + bias
+        peak = jnp.max(s, axis=1, keepdims=True)
+        e = jnp.exp(s - peak)
+        norm = jnp.sum(e, axis=1, keepdims=True)
+        o = mm(e.astype(BF), xp_ref[2, :, start : start + width] * mask) / norm
+        lse = jnp.where(lane == h, peak + jnp.log(norm), lse)
+        for part in range(width // LANES):
+            t = start // LANES + part
+            piece = o[:, part * LANES : (part + 1) * LANES]
+            total[t] = piece if total[t] is None else total[t] + piece
+    for t, value in enumerate(total):
+        o_ref[:, t * LANES : (t + 1) * LANES] = value
+    lse_ref[...] = lse
+
+
+def owner_fwd(q, k, v, heads):
+    rows = q.shape[0]
+    lane = iota2((rows, LANES), 1)
+    lse = jnp.full((rows, LANES), NEGATIVE_FILL, F32)
+    out = jnp.zeros((rows, LANES), F32)
+    for e in range(heads):
+        mask = lane_mask(LANES, HEAD * e, HEAD * (e + 1), HEAD * heads)
+        s = mm_t(q * mask, k) * SCALE
+        peak = jnp.max(s, axis=1, keepdims=True)
+        weights = jnp.exp(s - peak)
+        norm = jnp.sum(weights, axis=1, keepdims=True)
+        part = mm(weights.astype(BF), v * lane_mask(LANES, HEAD * e, HEAD * (e + 1)))
+        out = out + part / norm
+        lse = jnp.where(lane == e, peak + jnp.log(norm), lse)
+    return out, lse
+
+
+def slide_members(ss_ref, sources):
+    wide = ss_ref[...].astype(F32)
+    return [
+        wide[:, 8 * a : 8 * a + 8].reshape(sources * 8, LANES).astype(BF) for a in range(4)
+    ]
+
+
+def owner_fwd_kernel(gr_ref, sr_ref, go_ref, so_ref):
+    groups, sources = gr_ref.shape[0], sr_ref.shape[0]
+    q, k, v = [gr_ref[:, a].reshape(groups * 32, LANES) for a in range(3)]
+    out, lse = owner_fwd(q, k, v, 2)
+    go_ref[:, 0] = out.reshape(groups, 32, LANES)
+    go_ref[:, 1] = lse.reshape(groups, 32, LANES)
+    q, k, v, _ = slide_members(sr_ref, sources)
+    out, lse = owner_fwd(q, k, v, 1)
+    so_ref[:, 0] = out.reshape(sources, 8, LANES)
+    so_ref[:, 1] = lse.reshape(sources, 8, LANES)
+
+
+def head_spread(transposed):
+    shape = (HEADS * HEAD, LANES) if transposed else (LANES, HEADS * HEAD)
+    head, col = (iota2(shape, 1), iota2(shape, 0)) if transposed else (iota2(shape, 0), iota2(shape, 1))
+    return ((col >= head * HEAD) & (col < head * HEAD + HEAD)).astype(F32).astype(BF)
+
+
+def combine_kernel(
+    copies, xp_ref, on_ref, ln_ref, go_ref, so_ref, att_ref, plane_t_ref, g2_ref, s2_ref, acc_ref
+):
+    lane32 = iota2((32, LANES), 1)
+    lane8 = iota2((8, LANES), 1)
+    near = ln_ref[...]
+    group_rows, slide_rows = [], [None] * HEADS
+    for o in range(4):
+        pieces = []
+        for p in (2 * o, 2 * o + 1):
+            moved = pltpu.roll(go_ref[p, 1], 2 * p, 1) if p else go_ref[p, 1]
+            keep = (lane32 >= 2 * p) & (lane32 < 2 * p + 2)
+            pieces.append(jnp.where(keep, moved, NEGATIVE_FILL))
+        group_rows.append(jnp.maximum(pieces[0], pieces[1]))
+    for r in range(HEADS):
+        moved = pltpu.roll(so_ref[r, 1], r, 1) if r else so_ref[r, 1]
+        slide_rows[slide_row(r) // 8] = jnp.where(lane8 == r, moved, NEGATIVE_FILL)
+    group = jnp.concatenate(group_rows, axis=0)
+    slide = jnp.concatenate(slide_rows, axis=0)
+    best = jnp.maximum(jnp.maximum(near, group), slide)
+    near_w, group_w, slide_w = jnp.exp(near - best), jnp.exp(group - best), jnp.exp(slide - best)
+    den = near_w + group_w + slide_w
+    lse = best + jnp.log(den)
+    spread = head_spread(False)
+    acc_ref[...] = jnp.zeros_like(acc_ref)
+    for p in range(HEADS // 2):
+        row = p // 2 * 32
+        start, width, shift = window(PAIR * p, PAIR)
+        acc_ref[0, row : row + 32, start : start + width] += mm(
+            go_ref[p, 0].astype(BF), shift_out(width, shift, PAIR)
+        )
+    for r in range(HEADS):
+        row = slide_row(r)
+        start, width, shift = window(HEAD * r, HEAD)
+        acc_ref[1, row : row + 8, start : start + width] += mm(
+            so_ref[r, 0].astype(BF), shift_out(width, shift, HEAD)
+        )
+    attended = (
+        on_ref[...] * split_mm(near_w / den, spread)
+        + acc_ref[0] * split_mm(group_w / den, spread)
+        + acc_ref[1] * split_mm(slide_w / den, spread)
+    ).astype(BF)
+    att_ref[...] = mm(permute_matrix(True), attended).astype(BF)
+    product = xp_ref[3].astype(F32) * attended.astype(F32)
+    delta = split_mm(product, head_spread(True))
+    lane = iota2((LANES, LANES), 1)
+    plane = jnp.where(lane < HEADS, lse, pltpu.roll(delta, HEADS, 1))
+    plane_t_ref[...] = plane.T
+    for p in range(HEADS // 2):
+        row = p // 2 * 32
+        block = plane[row : row + 32]
+        g2_ref[p] = pltpu.roll(block, LANES - 2 * p, 1) if p else block
+    for r in range(HEADS):
+        row = slide_row(r)
+        block = plane[row : row + 8]
+        block = pltpu.roll(block, LANES - r, 1) if r else block
+        for copy in range(copies):
+            s2_ref[copy * HEADS + r] = block
+
+
+def near_bwd_kernel(len_ref, xp_ref, plane_t_ref, grads_ref):
+    bias = key_bias(len_ref, 0)
+    tiles = HEADS * HEAD // LANES
+    totals = [[None] * tiles for _ in range(3)]
+    for h in range(HEADS):
+        start, width, shift = window(HEAD * h, HEAD)
+        mask = lane_mask(width, shift, shift + HEAD)
+        qm, km, vm, cm = [xp_ref[a, :, start : start + width] * mask for a in range(4)]
+        s = mm_t(km, qm) * SCALE + bias
+        weights = jnp.exp(s - plane_t_ref[h : h + 1, :])
+        dp = mm_t(vm, cm)
+        ds = (weights * (dp - plane_t_ref[HEADS + h : HEADS + h + 1, :])).astype(BF)
+        results = (t_mm(ds, km), mm(ds, qm), mm(weights.astype(BF), cm))
+        for index, value in enumerate(results):
+            for part in range(width // LANES):
+                t = start // LANES + part
+                piece = value[:, part * LANES : (part + 1) * LANES]
+                old = totals[index][t]
+                totals[index][t] = piece if old is None else old + piece
+    for index in range(3):
+        for t in range(tiles):
+            value = totals[index][t]
+            grads_ref[index, :, t * LANES : (t + 1) * LANES] = value * SCALE if index < 2 else value
+
+
+def owner_bwd(q, k, v, c, plane, heads):
+    plane_t = plane.T
+    sums = [None] * 3
+    for e in range(heads):
+        mask = lane_mask(LANES, HEAD * e, HEAD * (e + 1))
+        q_flag = q * lane_mask(LANES, HEAD * e, HEAD * (e + 1), HEAD * heads)
+        cm = c * mask
+        s = mm_t(k, q_flag) * SCALE
+        weights = jnp.exp(s - plane_t[e : e + 1, :])
+        dp = mm_t(v, cm)
+        ds = (weights * (dp - plane_t[HEADS + e : HEADS + e + 1, :])).astype(BF)
+        parts = (t_mm(ds, k * mask), mm(ds, q * mask), mm(weights.astype(BF), cm))
+        sums = [part if old is None else old + part for old, part in zip(sums, parts)]
+    return sums[0] * SCALE, sums[1] * SCALE, sums[2]
+
+
+def owner_bwd_kernel(gr_ref, sr_ref, gp_ref, sp_ref, go_ref, so_ref):
+    groups, sources = gr_ref.shape[0], sr_ref.shape[0]
+    members = [gr_ref[:, a].reshape(groups * 32, LANES) for a in range(4)]
+    grads = owner_bwd(*members, gp_ref[...].reshape(groups * 32, LANES), 2)
+    for a in range(3):
+        go_ref[:, a] = grads[a].reshape(groups, 32, LANES).astype(BF)
+    members = slide_members(sr_ref, sources)
+    grads = owner_bwd(*members, sp_ref[...].reshape(sources * 8, LANES), 1)
+    stacked = [grad.reshape(sources, 8, LANES) for grad in grads]
+    stacked.append(jnp.zeros((sources, 8, LANES), F32))
+    so_ref[...] = jnp.concatenate(stacked, axis=1).astype(BF)
+
+
+def final_kernel(near_ref, go_ref, so_ref, dq_ref, dk_ref, dv_ref, acc_ref):
+    acc_ref[...] = near_ref[...]
+    for p in range(HEADS // 2):
+        row = p // 2 * 32
+        start, width, shift = window(PAIR * p, PAIR)
+        moved = mm(go_ref[p].reshape(96, LANES), shift_out(width, shift, PAIR))
+        for a in range(3):
+            acc_ref[a, row : row + 32, start : start + width] += moved[32 * a : 32 * a + 32]
+    for r in range(HEADS):
+        row = slide_row(r)
+        start, width, shift = window(HEAD * r, HEAD)
+        moved = mm(so_ref[r], shift_out(width, shift, HEAD))
+        for a in range(3):
+            acc_ref[a, row : row + 8, start : start + width] += moved[8 * a : 8 * a + 8]
+    back = permute_matrix(True)
+    for a, ref in enumerate((dq_ref, dk_ref, dv_ref)):
+        ref[...] = mm(back, acc_ref[a].astype(BF)).astype(BF)
+
+
+def shaped(shape, dtype):
+    return jax.ShapeDtypeStruct(shape, dtype)
+
+
+def run(kernel, outs, args, scalars=0, scratch=(), flops=20_000_000):
+    in_specs = [pl.BlockSpec(memory_space=pltpu.SMEM)] * scalars
+    in_specs += [pl.BlockSpec(memory_space=pltpu.VMEM)] * (len(args) - scalars)
+    out_specs = jax.tree.map(lambda _: pl.BlockSpec(memory_space=pltpu.VMEM), outs)
+    return pl.pallas_call(
+        kernel,
+        out_shape=outs,
+        in_specs=in_specs,
+        out_specs=out_specs,
+        scratch_shapes=list(scratch),
+        cost_estimate=pl.CostEstimate(flops=flops, bytes_accessed=4_000_000, transcendentals=300_000),
+        compiler_params=pltpu.CompilerParams(vmem_limit_bytes=48 * 1024 * 1024),
+    )(*args)
+
+
+def fast_local(inner, devices, query_tiles, key_tiles, value_tiles, cotangent, row_lengths):
+    copies = devices // HEADS
+    tiles, width = query_tiles.shape
+    every = ("outer", "inner")
+
+    def swap(array, axes):
+        return lax.all_to_all(array, axes, split_axis=0, concat_axis=0, tiled=True)
+
+    xp, group_send, slide_send = run(
+        lambda *refs: prep_kernel(copies, *refs),
+        (
+            shaped((4, tiles, width), BF),
+            shaped((inner, 4, 32, LANES), BF),
+            shaped((devices, 32, LANES), BF),
+        ),
+        (row_lengths, query_tiles, key_tiles, value_tiles, cotangent),
+        scalars=1,
+    )
+    group_got = swap(group_send, "inner")
+    slide_got = swap(slide_send, every)
+    near_out, near_lse = run(
+        near_fwd_kernel,
+        (shaped((tiles, width), F32), shaped((tiles, LANES), F32)),
+        (row_lengths, xp),
+        scalars=1,
+    )
+    group_out, slide_out = run(
+        owner_fwd_kernel,
+        (shaped((inner, 2, 32, LANES), F32), shaped((devices, 2, 8, LANES), F32)),
+        (group_got, slide_got),
+    )
+    group_back = swap(group_out, "inner")
+    slide_back = swap(slide_out, every)
+    attended, plane_t, group_plane, slide_plane = run(
+        lambda *refs: combine_kernel(copies, *refs),
+        (
+            shaped((tiles, width), BF),
+            shaped((LANES, tiles), F32),
+            shaped((inner, 32, LANES), F32),
+            shaped((devices, 8, LANES), F32),
+        ),
+        (xp, near_out, near_lse, group_back, slide_back),
+        scratch=(pltpu.VMEM((2, tiles, width), F32),),
+    )
+    group_plane = swap(group_plane, "inner")
+    slide_plane = swap(slide_plane, every)
+    near_grads = run(
+        near_bwd_kernel, shaped((3, tiles, width), F32), (row_lengths, xp, plane_t), scalars=1
+    )
+    group_grads, slide_grads = run(
+        owner_bwd_kernel,
+        (shaped((inner, 3, 32, LANES), BF), shaped((devices, 32, LANES), BF)),
+        (group_got, slide_got, group_plane, slide_plane),
+    )
+    group_grads = swap(group_grads, "inner")
+    slide_grads = swap(slide_grads, every)
+    grads = run(
+        final_kernel,
+        tuple(shaped((tiles, width), BF) for _ in range(3)),
+        (near_grads, group_grads, slide_grads),
+        scratch=(pltpu.VMEM((3, tiles, width), F32),),
+    )
+    return (attended,) + tuple(grads)
+
+
 def solution(mesh):
-    in_specs = (
-        P(("outer", "inner"), None),
-        P(("outer", "inner"), None),
-        P(("outer", "inner"), None),
-        P(("outer", "inner"), None),
-        P(("outer", "inner")),
-    )
-    out_specs = (
-        P(("outer", "inner"), None),
-        P(("outer", "inner"), None),
-        P(("outer", "inner"), None),
-        P(("outer", "inner"), None),
-    )
-    return jax.shard_map(local, mesh=mesh, in_specs=in_specs, out_specs=out_specs, check_vma=False)
+    in_specs = (P(("outer", "inner"), None),) * 4 + (P(("outer", "inner")),)
+    out_specs = (P(("outer", "inner"), None),) * 4
+    inner = mesh.shape["inner"]
+    devices = inner * mesh.shape["outer"]
+
+    def step(*args):
+        small = 2 * inner == HEADS and devices % HEADS == 0 and devices <= 64
+        if small and args[0].shape == (LANES, HEADS * HEAD):
+            return fast_local(inner, devices, *args)
+        return local(*args)
+
+    return jax.shard_map(step, mesh=mesh, in_specs=in_specs, out_specs=out_specs, check_vma=False)

time: 625 us -> 113 us (0.18)
  blocking collectives: 317 us -> 72.4 us
  local copies, waits for them, and re-layouts: 133 us -> 4.36 us
  waiting for transfers between devices: 68.5 us -> 13.3 us
  starting transfers between devices: 44.9 us -> 5.87 us
  matrix products: 25.8 us -> 0 us
  between operations: 16.8 us -> 0.7 us
  Pallas kernels: 0 us -> 15.5 us
  other arithmetic: 14.8 us -> 0 us
    all_gather x10 -> x0, blocking collectives: 317 us -> none  [the longest x1 34.4 us: local(): lax.all_gather(group_key, 'inner', axis=2, tiled=True)]
    unnamed x631 -> x12, local copies, waits for them, and re-layouts: 80.9 us -> 4.36 us
    all_to_all x0 -> x6, blocking collectives: none -> 72.4 us  [swap(): return lax.all_to_all(array, axes, split_axis=0, concat_axis=0, tiled=True)]
    reduce_scatter x2 -> x0, waiting for transfers between devices: 53 us -> none  [the longest x1 53 us: local(): lax.psum_scatter(partial_key.astype(jnp.bfloat16), 'inner', scatter_dimen...]
    all_to_all x13 -> x2, starting transfers between devices: 44.8 us -> 5.87 us  [swap(): return lax.all_to_all(array, axes, split_axis=0, concat_axis=0, tiled=True)]
    dot_general x58 -> x0, matrix products: 25.8 us -> none  [the longest x9 6.22 us: branch_grads(): jnp.einsum('hqk,hdq->hdk', weights.astype(jnp.bfloat16), cotan_block, pre...]
    pallas_call x0 -> x7, Pallas kernels: none -> 15.5 us  [run(): pl.pallas_call(kernel, out_shape=outs, in_specs=in_specs, out_specs=out_s...]
    slice x25 -> x0, local copies, waits for them, and re-layouts: 13.3 us -> none  [the longest x14 8.65 us: select_rows(): folded[head_index, ..., int(offsets[head_index])]]
  transfers between devices with their start and end apart: 15 -> 2, of which waited for: 8 -> 2; matrix products, arithmetic and copies ran while one was open for 20% -> 0% of each run, Pallas kernels for 0% -> 7%
where the time goes in v1:
time: 113 us; the launch traced here: 112 us
  blocking collectives  72.4 us (64%)
  Pallas kernels  15.5 us (14%)
  waiting for transfers between devices  13.3 us (12%)
  starting transfers between devices  5.87 us (5%)
  local copies, waits for them, and re-layouts  4.36 us (4%)
    all_to_all x6, blocking collectives, swap(): return lax.all_to_all(array, axes, split_axis=0, concat_axis=0, tiled=True)  72.4 us
    pallas_call x7, Pallas kernels, run(): pl.pallas_call(kernel, out_shape=outs, in_specs=in_specs, out_specs=out_s...  15.5 us
    all_to_all x2, waiting for transfers between devices, swap(): return lax.all_to_all(array, axes, split_axis=0, concat_axis=0, tiled=True)  13.3 us
    all_to_all x2, starting transfers between devices, swap(): return lax.all_to_all(array, axes, split_axis=0, concat_axis=0, tiled=True)  5.87 us
    unnamed x12, local copies, waits for them, and re-layouts  4.36 us
  transfers between devices with their start and end apart: 2, of which 2 were waited for; matrix products, arithmetic and copies ran while one was open for 0% of the time, Pallas kernels for 7%

profile of v1, /device:TPU:0, one launch (start us, length us, event | category | flops | bytes accessed | tf_op | source)
XLA Modules:
  0.0 112.0 jit_solution(5637710618824815814)
XLA Ops:
  0.6 0.0 copy-start
  0.6 0.9 copy-done
  1.6 0.9 copy-done.1
  2.5 0.9 copy-done.2
  3.4 0.9 copy-done.3
  4.3 0.7 copy-done.4
  5.0 1.2 %shard_map.84 = (bf16[4,128,768]{2,1,0:T(8,128)(2,1)S(1)}, bf16[8,4,32,128]{3,2,1,0:T(8,128)(2,1)S(1)}, bf16[32,32,128]{2,1,0:T(8,128)(2,1)S(1)}) custom-call(s32[4]{0:T(128)S(1)} %copy-done.4, bf16[128,768]{1,0:T(8,128)(2,1)S(1)} %copy-done, bf16[128,768]{1,0:T(8,128)(2,1)S(1)} %copy-done.1, bf16[128,768]{1,0:T(8,128)(2,1)S(1)} %copy-done.2, ...), custom_call_target="tpu_custom_call" | custom-call | flops 20000000 | bytes 4000000 | tf_op jit(solution)/shard_map/pallas_call | solution.py:662
  6.2 16.0 %all_to_all.40.gr_ref = bf16[8,4,32,128]{3,2,1,0:T(8,128)(2,1)S(1)} all-to-all(bf16[8,4,32,128]{3,2,1,0:T(8,128)(2,1)S(1)} %get-tuple-element.23), channel_id=1, replica_groups=mesh['outer'=4,'inner'=8] {'inner'}, dimensions={0} | all-to-all | bytes 524288 | tf_op jit(solution)/shard_map/all_to_all | solution.py:679
  22.2 14.0 %all_to_all.41.sr_ref = bf16[32,32,128]{2,1,0:T(8,128)(2,1)S(1)} all-to-all(bf16[32,32,128]{2,1,0:T(8,128)(2,1)S(1)} %get-tuple-element.24), channel_id=1, replica_groups=mesh['outer'=4,'inner'=8] {'outer','inner'}, dimensions={0} | all-to-all | bytes 524288 | tf_op jit(solution)/shard_map/all_to_all | solution.py:679
  36.3 1.5 %shard_map.86 = (f32[8,2,32,128]{3,2,1,0:T(8,128)S(1)}, f32[32,2,8,128]{3,2,1,0:T(8,128)}) custom-call(bf16[8,4,32,128]{3,2,1,0:T(8,128)(2,1)S(1)} %all_to_all.40.gr_ref, bf16[32,32,128]{2,1,0:T(8,128)(2,1)S(1)} %all_to_all.41.sr_ref), custom_call_target="tpu_custom_call" | custom-call | flops 20000000 | bytes 4000000 | tf_op jit(solution)/shard_map/pallas_call | solution.py:662
  37.7 11.5 %all_to_all.42.refs_3_ = f32[8,2,32,128]{3,2,1,0:T(8,128)S(1)} all-to-all(f32[8,2,32,128]{3,2,1,0:T(8,128)S(1)} %get-tuple-element.25), channel_id=1, replica_groups=mesh['outer'=4,'inner'=8] {'inner'}, dimensions={0} | all-to-all | bytes 524288 | tf_op jit(solution)/shard_map/all_to_all | solution.py:679
  49.3 3.3 %all-to-all-start.3 = ((f32[32,2,8,128]{3,2,1,0:T(8,128)}), f32[32,2,8,128]{3,2,1,0:T(8,128)S(1)}, u32[]{:S(2)}, u32[]{:S(2)}) async-start(f32[32,2,8,128]{3,2,1,0:T(8,128)} %get-tuple-element.26), calls=%async_computation.3 | async-start | bytes 524288 | tf_op jit(solution)/shard_map/all_to_all | solution.py:679
  52.5 0.0 copy-done.5
  52.6 3.7 %shard_map.85 = (f32[128,768]{1,0:T(8,128)S(1)}, f32[128,128]{1,0:T(8,128)S(1)}) custom-call(s32[4]{0:T(128)S(1)} %copy-done.5, bf16[4,128,768]{2,1,0:T(8,128)(2,1)S(1)} %get-tuple-element.20.xp_ref.refs_0_), custom_call_target="tpu_custom_call" | custom-call | flops 20000000 | bytes 4000000 | tf_op jit(solution)/shard_map/pallas_call | solution.py:662
  56.2 7.0 %all-to-all-done.3.refs_4_ = f32[32,2,8,128]{3,2,1,0:T(8,128)S(1)} async-done(((f32[32,2,8,128]{3,2,1,0:T(8,128)}), f32[32,2,8,128]{3,2,1,0:T(8,128)S(1)}, u32[]{:S(2)}, u32[]{:S(2)}) %all-to-all-start.3) | async-done | bytes 262176 | tf_op jit(solution)/shard_map/all_to_all | solution.py:679
  63.2 1.7 %shard_map.87 = (bf16[128,768]{1,0:T(8,128)(2,1)}, f32[128,128]{1,0:T(8,128)S(1)}, f32[8,32,128]{2,1,0:T(8,128)S(1)}, f32[32,8,128]{2,1,0:T(8,128)S(1)}) custom-call(bf16[4,128,768]{2,1,0:T(8,128)(2,1)S(1)} %get-tuple-element.20.xp_ref.refs_0_, f32[128,768]{1,0:T(8,128)S(1)} %get-tuple-element.21.refs_1_, f32[128,128]{1,0:T(8,128)S(1)} %get-tuple-element.22.refs_2_, ...), custom_call_target="tpu_custom_call" | custom-call | flops 20000000 | bytes 4000000 | tf_op jit(solution)/shard_map/pallas_call | solution.py:662
  64.9 10.3 %all_to_all.43.gp_ref = f32[8,32,128]{2,1,0:T(8,128)S(1)} all-to-all(f32[8,32,128]{2,1,0:T(8,128)S(1)} %get-tuple-element.29), channel_id=1, replica_groups=mesh['outer'=4,'inner'=8] {'inner'}, dimensions={0} | all-to-all | bytes 262144 | tf_op jit(solution)/shard_map/all_to_all | solution.py:679
  75.2 9.4 %all_to_all.44.sp_ref = f32[32,8,128]{2,1,0:T(8,128)S(1)} all-to-all(f32[32,8,128]{2,1,0:T(8,128)S(1)} %get-tuple-element.30), channel_id=1, replica_groups=mesh['outer'=4,'inner'=8] {'outer','inner'}, dimensions={0} | all-to-all | bytes 262144 | tf_op jit(solution)/shard_map/all_to_all | solution.py:679
  84.7 1.8 %shard_map.89 = (bf16[8,3,32,128]{3,2,1,0:T(8,128)(2,1)S(1)}, bf16[32,32,128]{2,1,0:T(8,128)(2,1)}) custom-call(bf16[8,4,32,128]{3,2,1,0:T(8,128)(2,1)S(1)} %all_to_all.40.gr_ref, bf16[32,32,128]{2,1,0:T(8,128)(2,1)S(1)} %all_to_all.41.sr_ref, f32[8,32,128]{2,1,0:T(8,128)S(1)} %all_to_all.43.gp_ref, f32[32,8,128]{2,1,0:T(8,128)S(1)} %all_to_all.44.sp_ref), custom_call_target="tpu_custom_call" | custom-call | flops 20000000 | bytes 4000000 | tf_op jit(solution)/shard_map/pallas_call | solution.py:662
  86.5 11.1 %all_to_all.45.go_ref = bf16[8,3,32,128]{3,2,1,0:T(8,128)(2,1)S(1)} all-to-all(bf16[8,3,32,128]{3,2,1,0:T(8,128)(2,1)S(1)} %get-tuple-element.31), channel_id=1, replica_groups=mesh['outer'=4,'inner'=8] {'inner'}, dimensions={0} | all-to-all | bytes 393216 | tf_op jit(solution)/shard_map/all_to_all | solution.py:679
  97.5 2.6 %all-to-all-start.7 = ((bf16[32,32,128]{2,1,0:T(8,128)(2,1)}), bf16[32,32,128]{2,1,0:T(8,128)(2,1)S(1)}, u32[]{:S(2)}, u32[]{:S(2)}) async-start(bf16[32,32,128]{2,1,0:T(8,128)(2,1)} %get-tuple-element.32), calls=%async_computation.7 | async-start | bytes 524288 | tf_op jit(solution)/shard_map/all_to_all | solution.py:679
  100.1 4.3 %shard_map.88.near_ref = f32[3,128,768]{2,1,0:T(8,128)S(1)} custom-call(s32[4]{0:T(128)S(1)} %copy-done.5, bf16[4,128,768]{2,1,0:T(8,128)(2,1)S(1)} %get-tuple-element.20.xp_ref.refs_0_, f32[128,128]{1,0:T(8,128)S(1)} %get-tuple-element.28.plane_t_ref), custom_call_target="tpu_custom_call" | custom-call | flops 20000000 | bytes 4000000 | tf_op jit(solution)/shard_map/pallas_call | solution.py:662
  104.4 6.4 %all-to-all-done.7.so_ref = bf16[32,32,128]{2,1,0:T(8,128)(2,1)S(1)} async-done(((bf16[32,32,128]{2,1,0:T(8,128)(2,1)}), bf16[32,32,128]{2,1,0:T(8,128)(2,1)S(1)}, u32[]{:S(2)}, u32[]{:S(2)}) %all-to-all-start.7) | async-done | bytes 262176 | tf_op jit(solution)/shard_map/all_to_all | solution.py:679
  110.8 1.3 %shard_map.90 = (bf16[128,768]{1,0:T(8,128)(2,1)}, bf16[128,768]{1,0:T(8,128)(2,1)}, bf16[128,768]{1,0:T(8,128)(2,1)}) custom-call(f32[3,128,768]{2,1,0:T(8,128)S(1)} %shard_map.88.near_ref, bf16[8,3,32,128]{3,2,1,0:T(8,128)(2,1)S(1)} %all_to_all.45.go_ref, bf16[32,32,128]{2,1,0:T(8,128)(2,1)S(1)} %all-to-all-done.7.so_ref), custom_call_target="tpu_custom_call" | custom-call | flops 20000000 | bytes 4000000 | tf_op jit(solution)/shard_map/pallas_call | solution.py:662
  (5 shorter events, 0.0 us)
Async XLA Ops:
  0.6 0.9 copy-start
  1.6 0.9 copy-start.1
  2.5 0.9 copy-start.2
  3.4 0.9 copy-start.3
  4.3 0.7 copy-start.4
  22.2 30.3 %copy-start.5 = (s32[4]{0:T(128)S(1)}, s32[4]{0:T(128)}, u32[]{:S(2)}) copy-start(s32[4]{0:T(128)} %len_ref.3) | copy-start | bytes 52
  49.3 13.9 %all-to-all-start.3 = ((f32[32,2,8,128]{3,2,1,0:T(8,128)}), f32[32,2,8,128]{3,2,1,0:T(8,128)S(1)}, u32[]{:S(2)}, u32[]{:S(2)}) async-start(f32[32,2,8,128]{3,2,1,0:T(8,128)} %get-tuple-element.26), calls=%async_computation.3 | async-start | bytes 524288 | tf_op jit(solution)/shard_map/all_to_all | solution.py:679
  97.5 13.2 %all-to-all-start.7 = ((bf16[32,32,128]{2,1,0:T(8,128)(2,1)}), bf16[32,32,128]{2,1,0:T(8,128)(2,1)S(1)}, u32[]{:S(2)}, u32[]{:S(2)}) async-start(bf16[32,32,128]{2,1,0:T(8,128)(2,1)} %get-tuple-element.32), calls=%async_computation.7 | async-start | bytes 524288 | tf_op jit(solution)/shard_map/all_to_all | solution.py:679

commit v2 on v1

--- a/solution.py
+++ b/solution.py
@@ -413,7 +413,7 @@
     return mm(high, onehot) + mm(low, onehot)
 
 
-def prep_kernel(copies, len_ref, q_ref, k_ref, v_ref, c_ref, xp_ref, gs_ref, ss_ref):
+def prep_kernel(len_ref, q_ref, k_ref, v_ref, c_ref, xp_ref, gs_ref, ss_ref):
     perm = permute_matrix(False)
     xs = []
     for index, ref in enumerate((q_ref, k_ref, v_ref, c_ref)):
@@ -448,8 +448,7 @@
             ],
             axis=0,
         ).astype(BF)
-        for copy in range(copies):
-            ss_ref[copy * HEADS + r] = block
+        ss_ref[r] = block
 
 
 def near_fwd_kernel(len_ref, xp_ref, o_ref, lse_ref):
@@ -500,12 +499,16 @@
     ]
 
 
-def owner_fwd_kernel(gr_ref, sr_ref, go_ref, so_ref):
-    groups, sources = gr_ref.shape[0], sr_ref.shape[0]
+def group_fwd(gr_ref, go_ref):
+    groups = gr_ref.shape[0]
     q, k, v = [gr_ref[:, a].reshape(groups * 32, LANES) for a in range(3)]
     out, lse = owner_fwd(q, k, v, 2)
     go_ref[:, 0] = out.reshape(groups, 32, LANES)
     go_ref[:, 1] = lse.reshape(groups, 32, LANES)
+
+
+def slide_fwd(sr_ref, so_ref):
+    sources = sr_ref.shape[0]
     q, k, v, _ = slide_members(sr_ref, sources)
     out, lse = owner_fwd(q, k, v, 1)
     so_ref[:, 0] = out.reshape(sources, 8, LANES)
@@ -519,7 +522,7 @@
 
 
 def combine_kernel(
-    copies, xp_ref, on_ref, ln_ref, go_ref, so_ref, att_ref, plane_t_ref, g2_ref, s2_ref, acc_ref
+    xp_ref, on_ref, ln_ref, go_ref, so_ref, att_ref, plane_t_ref, g2_ref, s2_ref, acc_ref
 ):
     lane32 = iota2((32, LANES), 1)
     lane8 = iota2((8, LANES), 1)
@@ -542,7 +545,7 @@
     den = near_w + group_w + slide_w
     lse = best + jnp.log(den)
     spread = head_spread(False)
-    acc_ref[...] = jnp.zeros_like(acc_ref)
+    acc_ref[0:2] = jnp.zeros((2,) + acc_ref.shape[1:], F32)
     for p in range(HEADS // 2):
         row = p // 2 * 32
         start, width, shift = window(PAIR * p, PAIR)
@@ -574,8 +577,7 @@
         row = slide_row(r)
         block = plane[row : row + 8]
         block = pltpu.roll(block, LANES - r, 1) if r else block
-        for copy in range(copies):
-            s2_ref[copy * HEADS + r] = block
+        s2_ref[r] = block
 
 
 def near_bwd_kernel(len_ref, xp_ref, plane_t_ref, grads_ref):
@@ -619,12 +621,16 @@
     return sums[0] * SCALE, sums[1] * SCALE, sums[2]
 
 
-def owner_bwd_kernel(gr_ref, sr_ref, gp_ref, sp_ref, go_ref, so_ref):
-    groups, sources = gr_ref.shape[0], sr_ref.shape[0]
+def group_bwd(gr_ref, gp_ref, go_ref):
+    groups = gr_ref.shape[0]
     members = [gr_ref[:, a].reshape(groups * 32, LANES) for a in range(4)]
     grads = owner_bwd(*members, gp_ref[...].reshape(groups * 32, LANES), 2)
     for a in range(3):
         go_ref[:, a] = grads[a].reshape(groups, 32, LANES).astype(BF)
+
+
+def slide_bwd(sr_ref, sp_ref, so_ref):
+    sources = sr_ref.shape[0]
     members = slide_members(sr_ref, sources)
     grads = owner_bwd(*members, sp_ref[...].reshape(sources * 8, LANES), 1)
     stacked = [grad.reshape(sources, 8, LANES) for grad in grads]
@@ -651,88 +657,288 @@
         ref[...] = mm(back, acc_ref[a].astype(BF)).astype(BF)
 
 
-def shaped(shape, dtype):
-    return jax.ShapeDtypeStruct(shape, dtype)
-
-
-def run(kernel, outs, args, scalars=0, scratch=(), flops=20_000_000):
-    in_specs = [pl.BlockSpec(memory_space=pltpu.SMEM)] * scalars
-    in_specs += [pl.BlockSpec(memory_space=pltpu.VMEM)] * (len(args) - scalars)
-    out_specs = jax.tree.map(lambda _: pl.BlockSpec(memory_space=pltpu.VMEM), outs)
-    return pl.pallas_call(
-        kernel,
-        out_shape=outs,
-        in_specs=in_specs,
-        out_specs=out_specs,
-        scratch_shapes=list(scratch),
-        cost_estimate=pl.CostEstimate(flops=flops, bytes_accessed=4_000_000, transcendentals=300_000),
-        compiler_params=pltpu.CompilerParams(vmem_limit_bytes=48 * 1024 * 1024),
-    )(*args)
-
-
-def fast_local(inner, devices, query_tiles, key_tiles, value_tiles, cotangent, row_lengths):
-    copies = devices // HEADS
-    tiles, width = query_tiles.shape
-    every = ("outer", "inner")
-
-    def swap(array, axes):
-        return lax.all_to_all(array, axes, split_axis=0, concat_axis=0, tiled=True)
-
-    xp, group_send, slide_send = run(
-        lambda *refs: prep_kernel(copies, *refs),
-        (
-            shaped((4, tiles, width), BF),
-            shaped((inner, 4, 32, LANES), BF),
-            shaped((devices, 32, LANES), BF),
-        ),
-        (row_lengths, query_tiles, key_tiles, value_tiles, cotangent),
-        scalars=1,
-    )
-    group_got = swap(group_send, "inner")
-    slide_got = swap(slide_send, every)
-    near_out, near_lse = run(
-        near_fwd_kernel,
-        (shaped((tiles, width), F32), shaped((tiles, LANES), F32)),
-        (row_lengths, xp),
-        scalars=1,
-    )
-    group_out, slide_out = run(
-        owner_fwd_kernel,
-        (shaped((inner, 2, 32, LANES), F32), shaped((devices, 2, 8, LANES), F32)),
-        (group_got, slide_got),
-    )
-    group_back = swap(group_out, "inner")
-    slide_back = swap(slide_out, every)
-    attended, plane_t, group_plane, slide_plane = run(
-        lambda *refs: combine_kernel(copies, *refs),
-        (
-            shaped((tiles, width), BF),
-            shaped((LANES, tiles), F32),
-            shaped((inner, 32, LANES), F32),
-            shaped((devices, 8, LANES), F32),
-        ),
-        (xp, near_out, near_lse, group_back, slide_back),
-        scratch=(pltpu.VMEM((2, tiles, width), F32),),
-    )
-    group_plane = swap(group_plane, "inner")
-    slide_plane = swap(slide_plane, every)
-    near_grads = run(
-        near_bwd_kernel, shaped((3, tiles, width), F32), (row_lengths, xp, plane_t), scalars=1
-    )
-    group_grads, slide_grads = run(
-        owner_bwd_kernel,
-        (shaped((inner, 3, 32, LANES), BF), shaped((devices, 32, LANES), BF)),
-        (group_got, slide_got, group_plane, slide_plane),
-    )
-    group_grads = swap(group_grads, "inner")
-    slide_grads = swap(slide_grads, every)
-    grads = run(
-        final_kernel,
-        tuple(shaped((tiles, width), BF) for _ in range(3)),
-        (near_grads, group_grads, slide_grads),
-        scratch=(pltpu.VMEM((3, tiles, width), F32),),
-    )
-    return (attended,) + tuple(grads)
+MESH = pl.DeviceIdType.MESH
+
+
+def remote(src, dst, send_sem, recv_sem, outer, inner):
+    return pltpu.make_async_remote_copy(
+        src_ref=src,
+        dst_ref=dst,
+        send_sem=send_sem,
+        recv_sem=recv_sem,
+        device_id=(outer, inner),
+        device_id_type=MESH,
+    )
+
+
+class Group:
+    def __init__(self, inner, src, dst, send_sem, recv_sem):
+        self.inner, self.src, self.dst = inner, src, dst
+        self.send_sem, self.recv_sem = send_sem, recv_sem
+
+    def copy(self, step):
+        me = lax.axis_index("inner")
+        peer = lax.rem(me + step, self.inner)
+        return remote(
+            self.src.at[peer],
+            self.dst.at[me],
+            self.send_sem.at[step],
+            self.recv_sem.at[step],
+            lax.axis_index("outer"),
+            peer,
+        )
+
+    def start(self):
+        @pl.loop(1, self.inner)
+        def _(step):
+            self.copy(step).start()
+
+        me = lax.axis_index("inner")
+        self.dst[me] = self.src[me]
+
+    def wait_recv(self):
+        @pl.loop(1, self.inner)
+        def _(step):
+            self.copy(step).wait_recv()
+
+    def wait_send(self):
+        @pl.loop(1, self.inner)
+        def _(step):
+            self.copy(step).wait_send()
+
+
+def owner_of(head, inner):
+    return 2 * (head // inner), lax.rem(head, inner)
+
+
+class ToOwner:
+    def __init__(self, inner, devices, src, dst, send_sem, recv_sem):
+        self.inner, self.devices, self.src, self.dst = inner, devices, src, dst
+        self.send_sem, self.recv_sem = send_sem, recv_sem
+
+    def place(self):
+        return lax.axis_index("outer"), lax.axis_index("inner")
+
+    def copy(self, head):
+        outer, inner = self.place()
+        to_outer, to_inner = owner_of(head, self.inner)
+        me = outer * self.inner + inner
+        return remote(
+            self.src.at[head],
+            self.dst.at[me],
+            self.send_sem.at[head],
+            self.recv_sem.at[me],
+            to_outer,
+            to_inner,
+        )
+
+    def each(self, other, own):
+        outer, inner = self.place()
+        me = outer * self.inner + inner
+
+        @pl.loop(0, HEADS)
+        def _(step):
+            head = lax.rem(step + me, HEADS)
+            to_outer, to_inner = owner_of(head, self.inner)
+            at_home = (to_outer * self.inner + to_inner) == me
+
+            @pl.when(jnp.logical_not(at_home))
+            def _():
+                other(head)
+
+            if own is not None:
+
+                @pl.when(at_home)
+                def _():
+                    own(head, me)
+
+    def start(self):
+        def keep(head, me):
+            self.dst[me] = self.src[head]
+
+        self.each(lambda head: self.copy(head).start(), keep)
+
+    def wait_recv(self):
+        outer, inner = self.place()
+        me = outer * self.inner + inner
+
+        @pl.loop(0, self.devices)
+        def _(source):
+            @pl.when(source != me)
+            def _():
+                remote(
+                    self.src.at[0],
+                    self.dst.at[source],
+                    self.send_sem.at[0],
+                    self.recv_sem.at[source],
+                    source // self.inner,
+                    lax.rem(source, self.inner),
+                ).wait_recv()
+
+    def wait_send(self):
+        self.each(lambda head: self.copy(head).wait_send(), None)
+
+
+class FromOwner:
+    def __init__(self, inner, devices, src, dst, send_sem, recv_sem):
+        self.inner, self.devices, self.src, self.dst = inner, devices, src, dst
+        self.send_sem, self.recv_sem = send_sem, recv_sem
+
+    def copy(self, target):
+        outer, inner = lax.axis_index("outer"), lax.axis_index("inner")
+        head = outer // 2 * self.inner + inner
+        return remote(
+            self.src.at[target],
+            self.dst.at[head],
+            self.send_sem.at[target],
+            self.recv_sem.at[head],
+            target // self.inner,
+            lax.rem(target, self.inner),
+        )
+
+    def start(self):
+        outer, inner = lax.axis_index("outer"), lax.axis_index("inner")
+        me = outer * self.inner + inner
+
+        @pl.loop(1, self.devices)
+        def _(step):
+            self.copy(lax.rem(me + step, self.devices)).start()
+
+        self.dst[outer // 2 * self.inner + inner] = self.src[me]
+
+    def wait_recv(self):
+        me = lax.axis_index("outer") * self.inner + lax.axis_index("inner")
+
+        @pl.loop(0, HEADS)
+        def _(head):
+            from_outer, from_inner = owner_of(head, self.inner)
+
+            @pl.when((from_outer * self.inner + from_inner) != me)
+            def _():
+                remote(
+                    self.src.at[0],
+                    self.dst.at[head],
+                    self.send_sem.at[0],
+                    self.recv_sem.at[head],
+                    from_outer,
+                    from_inner,
+                ).wait_recv()
+
+    def wait_send(self):
+        me = lax.axis_index("outer") * self.inner + lax.axis_index("inner")
+
+        @pl.loop(1, self.devices)
+        def _(step):
+            self.copy(lax.rem(me + step, self.devices)).wait_send()
+
+
+def whole_kernel(inner, devices, len_ref, q_ref, k_ref, v_ref, c_ref, att_ref, dq_ref, dk_ref, dv_ref, *scratch):
+    (xp, near_out, near_lse, plane_t, near_grads, acc) = scratch[:6]
+    (g1s, g1r, s1s, s1r, g2s, g2r, s2s, s2r, g3s, g3r, s3s, s3r, g4s, g4r, s4s, s4r) = scratch[6:22]
+    group_send, group_recv, slide_send, slide_recv = scratch[22:]
+    outer, place = lax.axis_index("outer"), lax.axis_index("inner")
+    me = outer * inner + place
+    is_owner = lax.rem(outer, 2) == 0
+
+    def group_exchange(phase, src, dst):
+        return Group(inner, src, dst, group_send.at[phase], group_recv.at[phase])
+
+    def slide_exchange(kind, phase, src, dst):
+        return kind(inner, devices, src, dst, slide_send.at[phase], slide_recv.at[phase])
+
+    group1, slide1 = group_exchange(0, g1s, g1r), slide_exchange(ToOwner, 0, s1s, s1r)
+    group2, slide2 = group_exchange(1, g2s, g2r), slide_exchange(FromOwner, 1, s2s, s2r)
+    group3, slide3 = group_exchange(2, g3s, g3r), slide_exchange(ToOwner, 2, s3s, s3r)
+    group4, slide4 = group_exchange(3, g4s, g4r), slide_exchange(FromOwner, 3, s4s, s4r)
+
+    barrier = pltpu.get_barrier_semaphore()
+
+    @pl.loop(1, devices)
+    def _(step):
+        other = lax.rem(me + step, devices)
+        pl.semaphore_signal(
+            barrier,
+            inc=1,
+            device_id=(other // inner, lax.rem(other, inner)),
+            device_id_type=MESH,
+        )
+
+    prep_kernel(len_ref, q_ref, k_ref, v_ref, c_ref, xp, g1s, s1s)
+    pl.semaphore_wait(barrier, devices - 1)
+    slide1.start()
+    group1.start()
+    near_fwd_kernel(len_ref, xp, near_out, near_lse)
+
+    @pl.when(is_owner)
+    def _():
+        slide1.wait_recv()
+        slide_fwd(s1r, s2s)
+        slide2.start()
+
+    group1.wait_recv()
+    group_fwd(g1r, g2s)
+    group2.start()
+    group2.wait_recv()
+    slide2.wait_recv()
+    combine_kernel(xp, near_out, near_lse, g2r, s2r, att_ref, plane_t, g3s, s3s, acc)
+    slide3.start()
+    group3.start()
+    near_bwd_kernel(len_ref, xp, plane_t, near_grads)
+
+    @pl.when(is_owner)
+    def _():
+        slide3.wait_recv()
+        slide_bwd(s1r, s3r, s4s)
+        slide4.start()
+
+    group3.wait_recv()
+    group_bwd(g1r, g3r, g4s)
+    group4.start()
+    group4.wait_recv()
+    slide4.wait_recv()
+    final_kernel(near_grads, g4r, s4r, dq_ref, dk_ref, dv_ref, acc)
+    for sent in (group1, slide1, group2, group3, slide3, group4):
+        sent.wait_send()
+
+    @pl.when(is_owner)
+    def _():
+        slide2.wait_send()
+        slide4.wait_send()
+
+
+def fast_local(inner, devices, *args):
+    row_lengths, tiles_in = args[4], args[:4]
+    tiles, width = tiles_in[0].shape
+    vmem = pl.BlockSpec(memory_space=pltpu.VMEM)
+
+    def both(count, back, shape, dtype):
+        return [pltpu.VMEM((count,) + shape, dtype), pltpu.VMEM((back,) + shape, dtype)]
+
+    scratch = [
+        pltpu.VMEM((4, tiles, width), BF),
+        pltpu.VMEM((tiles, width), F32),
+        pltpu.VMEM((tiles, LANES), F32),
+        pltpu.VMEM((LANES, tiles), F32),
+        pltpu.VMEM((3, tiles, width), F32),
+        pltpu.VMEM((3, tiles, width), F32),
+    ]
+    scratch += both(inner, inner, (4, 32, LANES), BF) + both(HEADS, devices, (32, LANES), BF)
+    scratch += both(inner, inner, (2, 32, LANES), F32) + both(devices, HEADS, (2, 8, LANES), F32)
+    scratch += both(inner, inner, (32, LANES), F32) + both(HEADS, devices, (8, LANES), F32)
+    scratch += both(inner, inner, (3, 32, LANES), BF) + both(devices, HEADS, (32, LANES), BF)
+    scratch += [pltpu.SemaphoreType.DMA((4, inner))] * 2 + [pltpu.SemaphoreType.DMA((4, devices))] * 2
+    return tuple(
+        pl.pallas_call(
+            lambda *refs: whole_kernel(inner, devices, *refs),
+            out_shape=[jax.ShapeDtypeStruct((tiles, width), BF)] * 4,
+            in_specs=[pl.BlockSpec(memory_space=pltpu.SMEM)] + [vmem] * 4,
+            out_specs=[vmem] * 4,
+            scratch_shapes=scratch,
+            compiler_params=pltpu.CompilerParams(
+                collective_id=0, has_side_effects=True, vmem_limit_bytes=48 * 1024 * 1024
+            ),
+        )(row_lengths, *tiles_in)
+    )
 
 
 def solution(mesh):
@@ -742,8 +948,8 @@
     devices = inner * mesh.shape["outer"]
 
     def step(*args):
-        small = 2 * inner == HEADS and devices % HEADS == 0 and devices <= 64
-        if small and args[0].shape == (LANES, HEADS * HEAD):
+        owners = 2 * inner == HEADS and devices == 2 * HEADS
+        if owners and args[0].shape == (LANES, HEADS * HEAD):
             return fast_local(inner, devices, *args)
         return local(*args)
 

time: 113 us -> 55.6 us (0.49)
  blocking collectives: 72.4 us -> 0 us
  Pallas kernels: 15.5 us -> 47.6 us
  waiting for transfers between devices: 13.3 us -> 0 us
  starting transfers between devices: 5.87 us -> 0 us
  local copies, waits for them, and re-layouts: 4.36 us -> 7.06 us
    all_to_all x6 -> x0, blocking collectives: 72.4 us -> none  [swap(): return lax.all_to_all(array, axes, split_axis=0, concat_axis=0, tiled=True)]
    pallas_call x7 -> x1, Pallas kernels: 15.5 us -> 47.6 us  [fast_local(): pl.pallas_call(lambda *refs: whole_kernel(inner, devices, *refs), out_sha...]
    all_to_all x2 -> x0, waiting for transfers between devices: 13.3 us -> none  [swap(): return lax.all_to_all(array, axes, split_axis=0, concat_axis=0, tiled=True)]
    all_to_all x2 -> x0, starting transfers between devices: 5.87 us -> none  [swap(): return lax.all_to_all(array, axes, split_axis=0, concat_axis=0, tiled=True)]
    unnamed x12 -> x14, local copies, waits for them, and re-layouts: 4.36 us -> 7.06 us
  transfers between devices with their start and end apart: 2 -> 0, of which waited for: 2 -> 0; matrix products, arithmetic and copies ran while one was open for 0% -> 0% of each run, Pallas kernels for 7% -> 0%
where the time goes in v2:
time: 55.6 us; the launch traced here: 55.3 us
  Pallas kernels  47.6 us (86%)
  local copies, waits for them, and re-layouts  7.06 us (13%)
  between operations  0.65 us (1%)
    pallas_call x1, Pallas kernels, fast_local(): pl.pallas_call(lambda *refs: whole_kernel(inner, devices, *refs), out_sha...  47.6 us
    unnamed x14, local copies, waits for them, and re-layouts  7.06 us

profile of v2, /device:TPU:0, one launch (start us, length us, event | category | flops | bytes accessed | tf_op | source)
XLA Modules:
  0.0 55.3 jit_solution(16784152343394242020)
XLA Ops:
  0.6 0.0 copy-start
  0.6 0.9 %copy-done = bf16[128,768]{1,0:T(8,128)(2,1)S(1)} copy-done((bf16[128,768]{1,0:T(8,128)(2,1)S(1)}, bf16[128,768]{1,0:T(8,128)(2,1)}, u32[]{:S(2)}) %copy-start) | copy-done | bytes 196632
  1.6 0.0 copy-start.1
  1.6 0.9 %copy-done.1 = bf16[128,768]{1,0:T(8,128)(2,1)S(1)} copy-done((bf16[128,768]{1,0:T(8,128)(2,1)S(1)}, bf16[128,768]{1,0:T(8,128)(2,1)}, u32[]{:S(2)}) %copy-start.1) | copy-done | bytes 196632
  2.5 0.0 copy-start.2
  2.5 0.9 %copy-done.2 = bf16[128,768]{1,0:T(8,128)(2,1)S(1)} copy-done((bf16[128,768]{1,0:T(8,128)(2,1)S(1)}, bf16[128,768]{1,0:T(8,128)(2,1)}, u32[]{:S(2)}) %copy-start.2) | copy-done | bytes 196632
  3.4 0.0 copy-start.3
  3.4 0.9 %copy-done.3 = bf16[128,768]{1,0:T(8,128)(2,1)S(1)} copy-done((bf16[128,768]{1,0:T(8,128)(2,1)S(1)}, bf16[128,768]{1,0:T(8,128)(2,1)}, u32[]{:S(2)}) %copy-start.3) | copy-done | bytes 196632
  4.3 0.0 copy-start.4
  4.3 0.7 %copy-done.4 = s32[4]{0:T(128)S(1)} copy-done((s32[4]{0:T(128)S(1)}, s32[4]{0:T(128)}, u32[]{:S(2)}) %copy-start.4) | copy-done | bytes 40
  5.0 47.6 %shard_map.84 = (bf16[128,768]{1,0:T(8,128)(2,1)S(1)}, bf16[128,768]{1,0:T(8,128)(2,1)S(1)}, bf16[128,768]{1,0:T(8,128)(2,1)S(1)}, bf16[128,768]{1,0:T(8,128)(2,1)S(1)}) custom-call(s32[4]{0:T(128)S(1)} %copy-done.4, bf16[128,768]{1,0:T(8,128)(2,1)S(1)} %copy-done, bf16[128,768]{1,0:T(8,128)(2,1)S(1)} %copy-done.1, bf16[128,768]{1,0:T(8,128)(2,1)S(1)} %copy-done.2, ...), custom_call_target="tpu_custom_call" | custom-call | tf_op jit(solution)/shard_map/pallas_call | solution.py:931
  52.6 0.7 %copy.13 = bf16[128,768]{1,0:T(8,128)(2,1)} copy(bf16[128,768]{1,0:T(8,128)(2,1)S(1)} %get-tuple-element.8) | data formatting | bytes 393216
  53.3 0.7 %copy.14 = bf16[128,768]{1,0:T(8,128)(2,1)} copy(bf16[128,768]{1,0:T(8,128)(2,1)S(1)} %get-tuple-element.9) | data formatting | bytes 393216
  54.0 0.7 %copy.15 = bf16[128,768]{1,0:T(8,128)(2,1)} copy(bf16[128,768]{1,0:T(8,128)(2,1)S(1)} %get-tuple-element.10) | data formatting | bytes 393216
  54.7 0.7 %copy.16 = bf16[128,768]{1,0:T(8,128)(2,1)} copy(bf16[128,768]{1,0:T(8,128)(2,1)S(1)} %get-tuple-element.11) | data formatting | bytes 393216
Async XLA Ops:
  0.6 0.9 %copy-start = (bf16[128,768]{1,0:T(8,128)(2,1)S(1)}, bf16[128,768]{1,0:T(8,128)(2,1)}, u32[]{:S(2)}) copy-start(bf16[128,768]{1,0:T(8,128)(2,1)} %refs_1_.1) | copy-start | bytes 589828
  1.6 0.9 %copy-start.1 = (bf16[128,768]{1,0:T(8,128)(2,1)S(1)}, bf16[128,768]{1,0:T(8,128)(2,1)}, u32[]{:S(2)}) copy-start(bf16[128,768]{1,0:T(8,128)(2,1)} %refs_2_.1) | copy-start | bytes 589828
  2.5 0.9 %copy-start.2 = (bf16[128,768]{1,0:T(8,128)(2,1)S(1)}, bf16[128,768]{1,0:T(8,128)(2,1)}, u32[]{:S(2)}) copy-start(bf16[128,768]{1,0:T(8,128)(2,1)} %refs_3_.1) | copy-start | bytes 589828
  3.4 0.9 %copy-start.3 = (bf16[128,768]{1,0:T(8,128)(2,1)S(1)}, bf16[128,768]{1,0:T(8,128)(2,1)}, u32[]{:S(2)}) copy-start(bf16[128,768]{1,0:T(8,128)(2,1)} %refs_4_.1) | copy-start | bytes 589828
  4.3 0.7 %copy-start.4 = (s32[4]{0:T(128)S(1)}, s32[4]{0:T(128)}, u32[]{:S(2)}) copy-start(s32[4]{0:T(128)} %refs_0_.1) | copy-start | bytes 52

commit v3 on v2

--- a/solution.py
+++ b/solution.py
@@ -342,6 +342,7 @@
 LANES = 128
 SCALE = HEAD ** (-0.5)
 PAIR = 2 * HEAD
+UPPER = LANES // 2
 
 
 def window(first_col, width):
@@ -373,14 +374,14 @@
     return jnp.where((tile & 31) < length, 0.0, NEGATIVE_FILL).astype(F32)
 
 
-def shift_in(width, shift, kept):
+def shift_in(width, shift, kept, base=0):
     row, col = iota2((width, LANES), 0), iota2((width, LANES), 1)
-    return ((row - shift == col) & (col < kept)).astype(F32).astype(BF)
-
-
-def shift_out(width, shift, kept):
+    return ((row - shift + base == col) & (col >= base) & (col < base + kept)).astype(F32).astype(BF)
+
+
+def shift_out(width, shift, kept, base=0):
     row, col = iota2((LANES, width), 0), iota2((LANES, width), 1)
-    return ((col - shift == row) & (row < kept)).astype(F32).astype(BF)
+    return ((col - shift + base == row) & (row >= base) & (row < base + kept)).astype(F32).astype(BF)
 
 
 def lane_mask(width, first, last, extra=-1):
@@ -413,7 +414,7 @@
     return mm(high, onehot) + mm(low, onehot)
 
 
-def prep_kernel(len_ref, q_ref, k_ref, v_ref, c_ref, xp_ref, gs_ref, ss_ref):
+def prep_kernel(len_ref, q_ref, k_ref, v_ref, c_ref, xp_ref, gs_ref, gc_ref, ss_ref):
     perm = permute_matrix(False)
     xs = []
     for index, ref in enumerate((q_ref, k_ref, v_ref, c_ref)):
@@ -431,24 +432,19 @@
         gs_ref[p, 0] = jnp.where(flag, 1.0, moved[0:32]).astype(BF)
         gs_ref[p, 1] = jnp.where(flag, bias[row : row + 32], moved[32:64]).astype(BF)
         gs_ref[p, 2] = moved[64:96].astype(BF)
-        gs_ref[p, 3] = moved[96:128].astype(BF)
+        gc_ref[p] = moved[96:128].astype(BF)
     for r in range(HEADS):
         row = slide_row(r)
         start, width, shift = window(HEAD * r, HEAD)
-        stacked = jnp.concatenate(
-            [x[row : row + 8, start : start + width] for x in xs], axis=0
-        ).astype(BF)
-        moved = mm(stacked, shift_in(width, shift, HEAD))
-        flag = iota2((8, LANES), 1) == HEAD
-        block = jnp.concatenate(
-            [
-                jnp.where(flag, 1.0, moved[0:8]),
-                jnp.where(flag, bias[row : row + 8], moved[8:16]),
-                moved[16:32],
-            ],
-            axis=0,
-        ).astype(BF)
-        ss_ref[r] = block
+        low, high = [
+            jnp.concatenate(
+                [xs[a][row : row + 8, start : start + width] for a in pair], axis=0
+            ).astype(BF)
+            for pair in ((0, 1), (3, 2))
+        ]
+        moved = mm(low, shift_in(width, shift, HEAD)) + mm(high, shift_in(width, shift, HEAD, UPPER))
+        flags = jnp.concatenate([jnp.ones((8, LANES), F32), bias[row : row + 8]], axis=0)
+        ss_ref[r] = jnp.where(iota2((16, LANES), 1) == HEAD, flags, moved).astype(BF)
 
 
 def near_fwd_kernel(len_ref, xp_ref, o_ref, lse_ref):
@@ -475,44 +471,51 @@
     lse_ref[...] = lse
 
 
-def owner_fwd(q, k, v, heads):
-    rows = q.shape[0]
-    lane = iota2((rows, LANES), 1)
-    lse = jnp.full((rows, LANES), NEGATIVE_FILL, F32)
-    out = jnp.zeros((rows, LANES), F32)
-    for e in range(heads):
-        mask = lane_mask(LANES, HEAD * e, HEAD * (e + 1), HEAD * heads)
-        s = mm_t(q * mask, k) * SCALE
-        peak = jnp.max(s, axis=1, keepdims=True)
-        weights = jnp.exp(s - peak)
-        norm = jnp.sum(weights, axis=1, keepdims=True)
-        part = mm(weights.astype(BF), v * lane_mask(LANES, HEAD * e, HEAD * (e + 1)))
-        out = out + part / norm
-        lse = jnp.where(lane == e, peak + jnp.log(norm), lse)
-    return out, lse
-
-
-def slide_members(ss_ref, sources):
-    wide = ss_ref[...].astype(F32)
-    return [
-        wide[:, 8 * a : 8 * a + 8].reshape(sources * 8, LANES).astype(BF) for a in range(4)
-    ]
+def three_parts(value):
+    high = value.astype(BF).astype(F32)
+    rest = value - high
+    middle = rest.astype(BF).astype(F32)
+    return high, middle, rest - middle
+
+
+def attend(q, k, v):
+    s = mm_t(q, k) * SCALE
+    peak = jnp.max(s, axis=1, keepdims=True)
+    weights = jnp.exp(s - peak)
+    norm = jnp.sum(weights, axis=1, keepdims=True)
+    return mm(weights.astype(BF), v) / norm, three_parts(peak + jnp.log(norm))
 
 
 def group_fwd(gr_ref, go_ref):
     groups = gr_ref.shape[0]
     q, k, v = [gr_ref[:, a].reshape(groups * 32, LANES) for a in range(3)]
-    out, lse = owner_fwd(q, k, v, 2)
-    go_ref[:, 0] = out.reshape(groups, 32, LANES)
-    go_ref[:, 1] = lse.reshape(groups, 32, LANES)
+    lane = iota2((groups * 32, LANES), 1)
+    total = None
+    for e in range(2):
+        mask = lane_mask(LANES, HEAD * e, HEAD * (e + 1))
+        out, parts = attend(q * lane_mask(LANES, HEAD * e, HEAD * (e + 1), PAIR), k, v * mask)
+        for index, part in enumerate(parts):
+            out = jnp.where(lane == PAIR + 2 * index + e, part, out)
+        total = out if total is None else total + out
+    go_ref[...] = total.astype(BF).reshape(groups, 32, LANES)
+
+
+def slide_members(sr_ref):
+    sources = sr_ref.shape[0]
+    wide = sr_ref[...].astype(F32)
+    return [wide[:, a : a + 8].reshape(sources * 8, LANES).astype(BF) for a in (0, 8)]
 
 
 def slide_fwd(sr_ref, so_ref):
     sources = sr_ref.shape[0]
-    q, k, v, _ = slide_members(sr_ref, sources)
-    out, lse = owner_fwd(q, k, v, 1)
-    so_ref[:, 0] = out.reshape(sources, 8, LANES)
-    so_ref[:, 1] = lse.reshape(sources, 8, LANES)
+    qc, kv = slide_members(sr_ref)
+    out, parts = attend(
+        qc * lane_mask(LANES, 0, HEAD + 1), kv, kv * lane_mask(LANES, UPPER, UPPER + HEAD)
+    )
+    lane = iota2((sources * 8, LANES), 1)
+    for index, part in enumerate(parts):
+        out = jnp.where(lane == index, part, out)
+    so_ref[...] = out.reshape(sources, 8, LANES).astype(BF)
 
 
 def head_spread(transposed):
@@ -531,12 +534,16 @@
     for o in range(4):
         pieces = []
         for p in (2 * o, 2 * o + 1):
-            moved = pltpu.roll(go_ref[p, 1], 2 * p, 1) if p else go_ref[p, 1]
+            block = go_ref[p].astype(F32)
+            block = block + pltpu.roll(block, LANES - 2, 1) + pltpu.roll(block, LANES - 4, 1)
+            moved = pltpu.roll(block, LANES - PAIR + 2 * p, 1)
             keep = (lane32 >= 2 * p) & (lane32 < 2 * p + 2)
             pieces.append(jnp.where(keep, moved, NEGATIVE_FILL))
         group_rows.append(jnp.maximum(pieces[0], pieces[1]))
     for r in range(HEADS):
-        moved = pltpu.roll(so_ref[r, 1], r, 1) if r else so_ref[r, 1]
+        block = so_ref[r].astype(F32)
+        block = block + pltpu.roll(block, LANES - 1, 1) + pltpu.roll(block, LANES - 2, 1)
+        moved = pltpu.roll(block, r, 1) if r else block
         slide_rows[slide_row(r) // 8] = jnp.where(lane8 == r, moved, NEGATIVE_FILL)
     group = jnp.concatenate(group_rows, axis=0)
     slide = jnp.concatenate(slide_rows, axis=0)
@@ -550,13 +557,13 @@
         row = p // 2 * 32
         start, width, shift = window(PAIR * p, PAIR)
         acc_ref[0, row : row + 32, start : start + width] += mm(
-            go_ref[p, 0].astype(BF), shift_out(width, shift, PAIR)
+            go_ref[p], shift_out(width, shift, PAIR)
         )
     for r in range(HEADS):
         row = slide_row(r)
         start, width, shift = window(HEAD * r, HEAD)
         acc_ref[1, row : row + 8, start : start + width] += mm(
-            so_ref[r, 0].astype(BF), shift_out(width, shift, HEAD)
+            so_ref[r], shift_out(width, shift, HEAD, UPPER)
         )
     attended = (
         on_ref[...] * split_mm(near_w / den, spread)
@@ -568,16 +575,20 @@
     delta = split_mm(product, head_spread(True))
     lane = iota2((LANES, LANES), 1)
     plane = jnp.where(lane < HEADS, lse, pltpu.roll(delta, HEADS, 1))
-    plane_t_ref[...] = plane.T
+    turned = plane.T
+    plane_t_ref[...] = turned
+    turned = turned[: 2 * HEADS]
+    g2_ref[...] = jnp.zeros_like(g2_ref)
+    s2_ref[...] = jnp.zeros_like(s2_ref)
     for p in range(HEADS // 2):
-        row = p // 2 * 32
-        block = plane[row : row + 32]
-        g2_ref[p] = pltpu.roll(block, LANES - 2 * p, 1) if p else block
+        moved = pltpu.roll(turned, LANES - p // 2 * 32, 1) if p >= 2 else turned
+        g2_ref[p, 0:2] = moved[2 * p : 2 * p + 2]
+        g2_ref[p, 2:4] = moved[HEADS + 2 * p : HEADS + 2 * p + 2]
     for r in range(HEADS):
         row = slide_row(r)
-        block = plane[row : row + 8]
-        block = pltpu.roll(block, LANES - r, 1) if r else block
-        s2_ref[r] = block
+        moved = pltpu.roll(turned, LANES - row, 1) if row else turned
+        s2_ref[r, 0:1] = moved[r : r + 1]
+        s2_ref[r, 1:2] = moved[HEADS + r : HEADS + r + 1]
 
 
 def near_bwd_kernel(len_ref, xp_ref, plane_t_ref, grads_ref):
@@ -605,36 +616,53 @@
             grads_ref[index, :, t * LANES : (t + 1) * LANES] = value * SCALE if index < 2 else value
 
 
-def owner_bwd(q, k, v, c, plane, heads):
-    plane_t = plane.T
+def join_rows(ref, span):
+    sources, per = ref.shape[0], LANES // span
+    lane = iota2((8, LANES), 1)
+    rows = []
+    for first in range(0, sources, per):
+        row = ref[first]
+        for index in range(1, per):
+            moved = pltpu.roll(ref[first + index], index * span, 1)
+            row = jnp.where(lane >= index * span, moved, row)
+        rows.append(row)
+    return jnp.concatenate(rows, axis=1)
+
+
+def score_grads(q, k, v, c, lse, delta):
+    weights = jnp.exp(mm_t(k, q) * SCALE - lse)
+    return weights.astype(BF), (weights * (mm_t(v, c) - delta)).astype(BF)
+
+
+def group_bwd(gr_ref, gc_ref, gp_ref, go_ref):
+    groups = gr_ref.shape[0]
+    q, k, v = [gr_ref[:, a].reshape(groups * 32, LANES) for a in range(3)]
+    c = gc_ref[...].reshape(groups * 32, LANES)
+    plane = join_rows(gp_ref, 32)
     sums = [None] * 3
-    for e in range(heads):
+    for e in range(2):
         mask = lane_mask(LANES, HEAD * e, HEAD * (e + 1))
-        q_flag = q * lane_mask(LANES, HEAD * e, HEAD * (e + 1), HEAD * heads)
+        q_flag = q * lane_mask(LANES, HEAD * e, HEAD * (e + 1), PAIR)
         cm = c * mask
-        s = mm_t(k, q_flag) * SCALE
-        weights = jnp.exp(s - plane_t[e : e + 1, :])
-        dp = mm_t(v, cm)
-        ds = (weights * (dp - plane_t[HEADS + e : HEADS + e + 1, :])).astype(BF)
-        parts = (t_mm(ds, k * mask), mm(ds, q * mask), mm(weights.astype(BF), cm))
+        weights, ds = score_grads(q_flag, k, v, cm, plane[e : e + 1], plane[2 + e : 3 + e])
+        parts = (t_mm(ds, k * mask), mm(ds, q * mask), mm(weights, cm))
         sums = [part if old is None else old + part for old, part in zip(sums, parts)]
-    return sums[0] * SCALE, sums[1] * SCALE, sums[2]
-
-
-def group_bwd(gr_ref, gp_ref, go_ref):
-    groups = gr_ref.shape[0]
-    members = [gr_ref[:, a].reshape(groups * 32, LANES) for a in range(4)]
-    grads = owner_bwd(*members, gp_ref[...].reshape(groups * 32, LANES), 2)
-    for a in range(3):
-        go_ref[:, a] = grads[a].reshape(groups, 32, LANES).astype(BF)
+    for a, grad in enumerate((sums[0] * SCALE, sums[1] * SCALE, sums[2])):
+        go_ref[:, a] = grad.reshape(groups, 32, LANES).astype(BF)
 
 
 def slide_bwd(sr_ref, sp_ref, so_ref):
     sources = sr_ref.shape[0]
-    members = slide_members(sr_ref, sources)
-    grads = owner_bwd(*members, sp_ref[...].reshape(sources * 8, LANES), 1)
-    stacked = [grad.reshape(sources, 8, LANES) for grad in grads]
-    stacked.append(jnp.zeros((sources, 8, LANES), F32))
+    qc, kv = slide_members(sr_ref)
+    plane = join_rows(sp_ref, 8)
+    low = lane_mask(LANES, 0, HEAD)
+    cm = qc * lane_mask(LANES, UPPER, UPPER + HEAD)
+    weights, ds = score_grads(
+        qc * lane_mask(LANES, 0, HEAD + 1), kv, kv, cm, plane[0:1], plane[1:2]
+    )
+    query = t_mm(ds, kv * low) * SCALE
+    key_value = mm(ds, qc * low) * SCALE + mm(weights, cm)
+    stacked = [grad.reshape(sources, 8, LANES) for grad in (query, key_value)]
     so_ref[...] = jnp.concatenate(stacked, axis=1).astype(BF)
 
 
@@ -650,8 +678,9 @@
         row = slide_row(r)
         start, width, shift = window(HEAD * r, HEAD)
         moved = mm(so_ref[r], shift_out(width, shift, HEAD))
-        for a in range(3):
-            acc_ref[a, row : row + 8, start : start + width] += moved[8 * a : 8 * a + 8]
+        upper = mm(so_ref[r], shift_out(width, shift, HEAD, UPPER))
+        for a, piece in enumerate((moved[0:8], moved[8:16], upper[8:16])):
+            acc_ref[a, row : row + 8, start : start + width] += piece
     back = permute_matrix(True)
     for a, ref in enumerate((dq_ref, dk_ref, dv_ref)):
         ref[...] = mm(back, acc_ref[a].astype(BF)).astype(BF)
@@ -678,7 +707,7 @@
 
     def copy(self, step):
         me = lax.axis_index("inner")
-        peer = lax.rem(me + step, self.inner)
+        peer = wrapped(me + step, self.inner)
         return remote(
             self.src.at[peer],
             self.dst.at[me],
@@ -707,8 +736,13 @@
             self.copy(step).wait_send()
 
 
+def wrapped(value, count):
+    return jnp.where(value >= count, value - count, value)
+
+
 def owner_of(head, inner):
-    return 2 * (head // inner), lax.rem(head, inner)
+    high = jnp.where(head >= inner, 1, 0)
+    return 2 * high, head - inner * high
 
 
 class ToOwner:
@@ -736,9 +770,11 @@
         outer, inner = self.place()
         me = outer * self.inner + inner
 
+        first = wrapped(me, HEADS)
+
         @pl.loop(0, HEADS)
         def _(step):
-            head = lax.rem(step + me, HEADS)
+            head = wrapped(step + first, HEADS)
             to_outer, to_inner = owner_of(head, self.inner)
             at_home = (to_outer * self.inner + to_inner) == me
 
@@ -762,21 +798,36 @@
         outer, inner = self.place()
         me = outer * self.inner + inner
 
-        @pl.loop(0, self.devices)
-        def _(source):
-            @pl.when(source != me)
-            def _():
-                remote(
-                    self.src.at[0],
-                    self.dst.at[source],
-                    self.send_sem.at[0],
-                    self.recv_sem.at[source],
-                    source // self.inner,
-                    lax.rem(source, self.inner),
-                ).wait_recv()
+        for source_outer in range(self.devices // self.inner):
+
+            @pl.loop(0, self.inner)
+            def _(source_inner):
+                source = source_outer * self.inner + source_inner
+
+                @pl.when(source != me)
+                def _():
+                    remote(
+                        self.src.at[0],
+                        self.dst.at[source],
+                        self.send_sem.at[0],
+                        self.recv_sem.at[source],
+                        source_outer,
+                        source_inner,
+                    ).wait_recv()
 
     def wait_send(self):
         self.each(lambda head: self.copy(head).wait_send(), None)
+
+
+def others(inner, devices, act):
+    mine, me = lax.axis_index("outer"), lax.axis_index("inner")
+    count = devices // inner
+    for step in range(count):
+        to_outer = wrapped(mine + step, count)
+
+        @pl.loop(1 if step == 0 else 0, inner)
+        def _(place):
+            act(to_outer, wrapped(me + place, inner))
 
 
 class FromOwner:
@@ -784,7 +835,8 @@
         self.inner, self.devices, self.src, self.dst = inner, devices, src, dst
         self.send_sem, self.recv_sem = send_sem, recv_sem
 
-    def copy(self, target):
+    def copy(self, to_outer, to_inner):
+        target = to_outer * self.inner + to_inner
         outer, inner = lax.axis_index("outer"), lax.axis_index("inner")
         head = outer // 2 * self.inner + inner
         return remote(
@@ -792,18 +844,14 @@
             self.dst.at[head],
             self.send_sem.at[target],
             self.recv_sem.at[head],
-            target // self.inner,
-            lax.rem(target, self.inner),
+            to_outer,
+            to_inner,
         )
 
     def start(self):
         outer, inner = lax.axis_index("outer"), lax.axis_index("inner")
         me = outer * self.inner + inner
-
-        @pl.loop(1, self.devices)
-        def _(step):
-            self.copy(lax.rem(me + step, self.devices)).start()
-
+        others(self.inner, self.devices, lambda *place: self.copy(*place).start())
         self.dst[outer // 2 * self.inner + inner] = self.src[me]
 
     def wait_recv(self):
@@ -825,19 +873,15 @@
                 ).wait_recv()
 
     def wait_send(self):
-        me = lax.axis_index("outer") * self.inner + lax.axis_index("inner")
-
-        @pl.loop(1, self.devices)
-        def _(step):
-            self.copy(lax.rem(me + step, self.devices)).wait_send()
+        others(self.inner, self.devices, lambda *place: self.copy(*place).wait_send())
 
 
 def whole_kernel(inner, devices, len_ref, q_ref, k_ref, v_ref, c_ref, att_ref, dq_ref, dk_ref, dv_ref, *scratch):
     (xp, near_out, near_lse, plane_t, near_grads, acc) = scratch[:6]
+    staged, gcs, gcr, load_sem = scratch[26:]
     (g1s, g1r, s1s, s1r, g2s, g2r, s2s, s2r, g3s, g3r, s3s, s3r, g4s, g4r, s4s, s4r) = scratch[6:22]
-    group_send, group_recv, slide_send, slide_recv = scratch[22:]
+    group_send, group_recv, slide_send, slide_recv = scratch[22:26]
     outer, place = lax.axis_index("outer"), lax.axis_index("inner")
-    me = outer * inner + place
     is_owner = lax.rem(outer, 2) == 0
 
     def group_exchange(phase, src, dst):
@@ -851,22 +895,26 @@
     group3, slide3 = group_exchange(2, g3s, g3r), slide_exchange(ToOwner, 2, s3s, s3r)
     group4, slide4 = group_exchange(3, g4s, g4r), slide_exchange(FromOwner, 3, s4s, s4r)
 
+    group_c = group_exchange(4, gcs, gcr)
     barrier = pltpu.get_barrier_semaphore()
 
-    @pl.loop(1, devices)
-    def _(step):
-        other = lax.rem(me + step, devices)
-        pl.semaphore_signal(
-            barrier,
-            inc=1,
-            device_id=(other // inner, lax.rem(other, inner)),
-            device_id_type=MESH,
-        )
-
-    prep_kernel(len_ref, q_ref, k_ref, v_ref, c_ref, xp, g1s, s1s)
+    def greet(*other):
+        pl.semaphore_signal(barrier, inc=1, device_id=other, device_id_type=MESH)
+
+    loads = [
+        pltpu.make_async_copy(ref, staged.at[a], load_sem.at[a])
+        for a, ref in enumerate((q_ref, k_ref, v_ref, c_ref))
+    ]
+    for load in loads:
+        load.start()
+    others(inner, devices, greet)
+    for load in loads:
+        load.wait()
+    prep_kernel(len_ref, *[staged.at[a] for a in range(4)], xp, g1s, gcs, s1s)
     pl.semaphore_wait(barrier, devices - 1)
     slide1.start()
     group1.start()
+    group_c.start()
     near_fwd_kernel(len_ref, xp, near_out, near_lse)
 
     @pl.when(is_owner)
@@ -891,13 +939,14 @@
         slide_bwd(s1r, s3r, s4s)
         slide4.start()
 
+    group_c.wait_recv()
     group3.wait_recv()
-    group_bwd(g1r, g3r, g4s)
+    group_bwd(g1r, gcr, g3r, g4s)
     group4.start()
     group4.wait_recv()
     slide4.wait_recv()
     final_kernel(near_grads, g4r, s4r, dq_ref, dk_ref, dv_ref, acc)
-    for sent in (group1, slide1, group2, group3, slide3, group4):
+    for sent in (group1, slide1, group_c, group2, group3, slide3, group4):
         sent.wait_send()
 
     @pl.when(is_owner)
@@ -922,16 +971,18 @@
         pltpu.VMEM((3, tiles, width), F32),
         pltpu.VMEM((3, tiles, width), F32),
     ]
-    scratch += both(inner, inner, (4, 32, LANES), BF) + both(HEADS, devices, (32, LANES), BF)
-    scratch += both(inner, inner, (2, 32, LANES), F32) + both(devices, HEADS, (2, 8, LANES), F32)
-    scratch += both(inner, inner, (32, LANES), F32) + both(HEADS, devices, (8, LANES), F32)
-    scratch += both(inner, inner, (3, 32, LANES), BF) + both(devices, HEADS, (32, LANES), BF)
-    scratch += [pltpu.SemaphoreType.DMA((4, inner))] * 2 + [pltpu.SemaphoreType.DMA((4, devices))] * 2
+    scratch += both(inner, inner, (3, 32, LANES), BF) + both(HEADS, devices, (16, LANES), BF)
+    scratch += both(inner, inner, (32, LANES), BF) + both(devices, HEADS, (8, LANES), BF)
+    scratch += both(inner, inner, (8, LANES), F32) + both(HEADS, devices, (8, LANES), F32)
+    scratch += both(inner, inner, (3, 32, LANES), BF) + both(devices, HEADS, (16, LANES), BF)
+    scratch += [pltpu.SemaphoreType.DMA((5, inner))] * 2 + [pltpu.SemaphoreType.DMA((4, devices))] * 2
+    scratch += [pltpu.VMEM((4, tiles, width), BF)] + both(inner, inner, (32, LANES), BF)
+    scratch += [pltpu.SemaphoreType.DMA((4,))]
     return tuple(
         pl.pallas_call(
             lambda *refs: whole_kernel(inner, devices, *refs),
             out_shape=[jax.ShapeDtypeStruct((tiles, width), BF)] * 4,
-            in_specs=[pl.BlockSpec(memory_space=pltpu.SMEM)] + [vmem] * 4,
+            in_specs=[pl.BlockSpec(memory_space=pltpu.SMEM)] + [pl.BlockSpec(memory_space=pltpu.HBM)] * 4,
             out_specs=[vmem] * 4,
             scratch_shapes=scratch,
             compiler_params=pltpu.CompilerParams(

time: 55.6 us -> 47.9 us (0.86)
  Pallas kernels: 47.6 us -> 39.9 us
    pallas_call x1, Pallas kernels: 47.6 us -> 39.9 us  [fast_local(): pl.pallas_call(lambda *refs: whole_kernel(inner, devices, *refs), out_sha...]
where the time goes in v3:
time: 47.9 us; the launch traced here: 47.6 us
  Pallas kernels  39.9 us (83%)
  local copies, waits for them, and re-layouts  7.06 us (15%)
  between operations  0.65 us (1%)
    pallas_call x1, Pallas kernels, fast_local(): pl.pallas_call(lambda *refs: whole_kernel(inner, devices, *refs), out_sha...  39.9 us
    unnamed x14, local copies, waits for them, and re-layouts  7.06 us

profile of v3, /device:TPU:0, one launch (start us, length us, event | category | flops | bytes accessed | tf_op | source)
XLA Modules:
  0.0 47.6 jit_solution(11796964187915684385)
XLA Ops:
  0.6 0.0 copy-start
  0.6 0.9 %copy-done = bf16[128,768]{1,0:T(8,128)(2,1)S(1)} copy-done((bf16[128,768]{1,0:T(8,128)(2,1)S(1)}, bf16[128,768]{1,0:T(8,128)(2,1)}, u32[]{:S(2)}) %copy-start) | copy-done | bytes 196632
  1.6 0.0 copy-start.1
  1.6 0.9 %copy-done.1 = bf16[128,768]{1,0:T(8,128)(2,1)S(1)} copy-done((bf16[128,768]{1,0:T(8,128)(2,1)S(1)}, bf16[128,768]{1,0:T(8,128)(2,1)}, u32[]{:S(2)}) %copy-start.1) | copy-done | bytes 196632
  2.5 0.0 copy-start.2
  2.5 0.9 %copy-done.2 = bf16[128,768]{1,0:T(8,128)(2,1)S(1)} copy-done((bf16[128,768]{1,0:T(8,128)(2,1)S(1)}, bf16[128,768]{1,0:T(8,128)(2,1)}, u32[]{:S(2)}) %copy-start.2) | copy-done | bytes 196632
  3.4 0.0 copy-start.3
  3.4 0.9 %copy-done.3 = bf16[128,768]{1,0:T(8,128)(2,1)S(1)} copy-done((bf16[128,768]{1,0:T(8,128)(2,1)S(1)}, bf16[128,768]{1,0:T(8,128)(2,1)}, u32[]{:S(2)}) %copy-start.3) | copy-done | bytes 196632
  4.3 0.0 copy-start.4
  4.3 0.7 %copy-done.4 = s32[4]{0:T(128)S(1)} copy-done((s32[4]{0:T(128)S(1)}, s32[4]{0:T(128)}, u32[]{:S(2)}) %copy-start.4) | copy-done | bytes 40
  5.0 39.9 %shard_map.84 = (bf16[128,768]{1,0:T(8,128)(2,1)S(1)}, bf16[128,768]{1,0:T(8,128)(2,1)S(1)}, bf16[128,768]{1,0:T(8,128)(2,1)S(1)}, bf16[128,768]{1,0:T(8,128)(2,1)S(1)}) custom-call(s32[4]{0:T(128)S(1)} %copy-done.4, bf16[128,768]{1,0:T(8,128)(2,1)S(1)} %copy-done, bf16[128,768]{1,0:T(8,128)(2,1)S(1)} %copy-done.1, bf16[128,768]{1,0:T(8,128)(2,1)S(1)} %copy-done.2, ...), custom_call_target="tpu_custom_call" | custom-call | tf_op jit(solution)/shard_map/pallas_call | solution.py:982
  44.9 0.7 %copy.13 = bf16[128,768]{1,0:T(8,128)(2,1)} copy(bf16[128,768]{1,0:T(8,128)(2,1)S(1)} %get-tuple-element.8) | data formatting | bytes 393216
  45.6 0.7 %copy.14 = bf16[128,768]{1,0:T(8,128)(2,1)} copy(bf16[128,768]{1,0:T(8,128)(2,1)S(1)} %get-tuple-element.9) | data formatting | bytes 393216
  46.3 0.7 %copy.15 = bf16[128,768]{1,0:T(8,128)(2,1)} copy(bf16[128,768]{1,0:T(8,128)(2,1)S(1)} %get-tuple-element.10) | data formatting | bytes 393216
  47.0 0.7 %copy.16 = bf16[128,768]{1,0:T(8,128)(2,1)} copy(bf16[128,768]{1,0:T(8,128)(2,1)S(1)} %get-tuple-element.11) | data formatting | bytes 393216
Async XLA Ops:
  0.6 0.9 %copy-start = (bf16[128,768]{1,0:T(8,128)(2,1)S(1)}, bf16[128,768]{1,0:T(8,128)(2,1)}, u32[]{:S(2)}) copy-start(bf16[128,768]{1,0:T(8,128)(2,1)} %refs_1_.1) | copy-start | bytes 589828
  1.6 0.9 %copy-start.1 = (bf16[128,768]{1,0:T(8,128)(2,1)S(1)}, bf16[128,768]{1,0:T(8,128)(2,1)}, u32[]{:S(2)}) copy-start(bf16[128,768]{1,0:T(8,128)(2,1)} %refs_2_.1) | copy-start | bytes 589828
  2.5 0.9 %copy-start.2 = (bf16[128,768]{1,0:T(8,128)(2,1)S(1)}, bf16[128,768]{1,0:T(8,128)(2,1)}, u32[]{:S(2)}) copy-start(bf16[128,768]{1,0:T(8,128)(2,1)} %refs_3_.1) | copy-start | bytes 589828
  3.4 0.9 %copy-start.3 = (bf16[128,768]{1,0:T(8,128)(2,1)S(1)}, bf16[128,768]{1,0:T(8,128)(2,1)}, u32[]{:S(2)}) copy-start(bf16[128,768]{1,0:T(8,128)(2,1)} %refs_4_.1) | copy-start | bytes 589828
  4.3 0.7 %copy-start.4 = (s32[4]{0:T(128)S(1)}, s32[4]{0:T(128)}, u32[]{:S(2)}) copy-start(s32[4]{0:T(128)} %refs_0_.1) | copy-start | bytes 52

commit v4 on v3

--- a/solution.py
+++ b/solution.py
@@ -444,7 +444,7 @@
         ]
         moved = mm(low, shift_in(width, shift, HEAD)) + mm(high, shift_in(width, shift, HEAD, UPPER))
         flags = jnp.concatenate([jnp.ones((8, LANES), F32), bias[row : row + 8]], axis=0)
-        ss_ref[r] = jnp.where(iota2((16, LANES), 1) == HEAD, flags, moved).astype(BF)
+        ss_ref[r // 8, r % 8] = jnp.where(iota2((16, LANES), 1) == HEAD, flags, moved).astype(BF)
 
 
 def near_fwd_kernel(len_ref, xp_ref, o_ref, lse_ref):
@@ -501,13 +501,13 @@
 
 
 def slide_members(sr_ref):
-    sources = sr_ref.shape[0]
-    wide = sr_ref[...].astype(F32)
+    sources = sr_ref.shape[0] * sr_ref.shape[1]
+    wide = sr_ref[...].astype(F32).reshape(sources, 16, LANES)
     return [wide[:, a : a + 8].reshape(sources * 8, LANES).astype(BF) for a in (0, 8)]
 
 
 def slide_fwd(sr_ref, so_ref):
-    sources = sr_ref.shape[0]
+    sources = sr_ref.shape[0] * sr_ref.shape[1]
     qc, kv = slide_members(sr_ref)
     out, parts = attend(
         qc * lane_mask(LANES, 0, HEAD + 1), kv, kv * lane_mask(LANES, UPPER, UPPER + HEAD)
@@ -515,7 +515,7 @@
     lane = iota2((sources * 8, LANES), 1)
     for index, part in enumerate(parts):
         out = jnp.where(lane == index, part, out)
-    so_ref[...] = out.reshape(sources, 8, LANES).astype(BF)
+    so_ref[...] = out.reshape(so_ref.shape).astype(BF)
 
 
 def head_spread(transposed):
@@ -541,7 +541,7 @@
             pieces.append(jnp.where(keep, moved, NEGATIVE_FILL))
         group_rows.append(jnp.maximum(pieces[0], pieces[1]))
     for r in range(HEADS):
-        block = so_ref[r].astype(F32)
+        block = so_ref[r // 8, r % 8].astype(F32)
         block = block + pltpu.roll(block, LANES - 1, 1) + pltpu.roll(block, LANES - 2, 1)
         moved = pltpu.roll(block, r, 1) if r else block
         slide_rows[slide_row(r) // 8] = jnp.where(lane8 == r, moved, NEGATIVE_FILL)
@@ -563,7 +563,7 @@
         row = slide_row(r)
         start, width, shift = window(HEAD * r, HEAD)
         acc_ref[1, row : row + 8, start : start + width] += mm(
-            so_ref[r], shift_out(width, shift, HEAD, UPPER)
+            so_ref[r // 8, r % 8], shift_out(width, shift, HEAD, UPPER)
         )
     attended = (
         on_ref[...] * split_mm(near_w / den, spread)
@@ -587,8 +587,8 @@
     for r in range(HEADS):
         row = slide_row(r)
         moved = pltpu.roll(turned, LANES - row, 1) if row else turned
-        s2_ref[r, 0:1] = moved[r : r + 1]
-        s2_ref[r, 1:2] = moved[HEADS + r : HEADS + r + 1]
+        s2_ref[r // 8, r % 8, 0:1] = moved[r : r + 1]
+        s2_ref[r // 8, r % 8, 1:2] = moved[HEADS + r : HEADS + r + 1]
 
 
 def near_bwd_kernel(len_ref, xp_ref, plane_t_ref, grads_ref):
@@ -617,7 +617,10 @@
 
 
 def join_rows(ref, span):
-    sources, per = ref.shape[0], LANES // span
+    ref = [ref[i] for i in range(ref.shape[0])] if len(ref.shape) == 3 else [
+        ref[i, j] for i in range(ref.shape[0]) for j in range(ref.shape[1])
+    ]
+    sources, per = len(ref), LANES // span
     lane = iota2((8, LANES), 1)
     rows = []
     for first in range(0, sources, per):
@@ -652,7 +655,7 @@
 
 
 def slide_bwd(sr_ref, sp_ref, so_ref):
-    sources = sr_ref.shape[0]
+    sources = sr_ref.shape[0] * sr_ref.shape[1]
     qc, kv = slide_members(sr_ref)
     plane = join_rows(sp_ref, 8)
     low = lane_mask(LANES, 0, HEAD)
@@ -663,7 +666,7 @@
     query = t_mm(ds, kv * low) * SCALE
     key_value = mm(ds, qc * low) * SCALE + mm(weights, cm)
     stacked = [grad.reshape(sources, 8, LANES) for grad in (query, key_value)]
-    so_ref[...] = jnp.concatenate(stacked, axis=1).astype(BF)
+    so_ref[...] = jnp.concatenate(stacked, axis=1).reshape(so_ref.shape).astype(BF)
 
 
 def final_kernel(near_ref, go_ref, so_ref, dq_ref, dk_ref, dv_ref, acc_ref):
@@ -677,8 +680,8 @@
     for r in range(HEADS):
         row = slide_row(r)
         start, width, shift = window(HEAD * r, HEAD)
-        moved = mm(so_ref[r], shift_out(width, shift, HEAD))
-        upper = mm(so_ref[r], shift_out(width, shift, HEAD, UPPER))
+        moved = mm(so_ref[r // 8, r % 8], shift_out(width, shift, HEAD))
+        upper = mm(so_ref[r // 8, r % 8], shift_out(width, shift, HEAD, UPPER))
         for a, piece in enumerate((moved[0:8], moved[8:16], upper[8:16])):
             acc_ref[a, row : row + 8, start : start + width] += piece
     back = permute_matrix(True)
@@ -701,7 +704,8 @@
 
 
 class Group:
-    def __init__(self, inner, src, dst, send_sem, recv_sem):
+    def __init__(self, inner, src, dst, send_sem, recv_sem, second=False):
+        self.second = second
         self.inner, self.src, self.dst = inner, src, dst
         self.send_sem, self.recv_sem = send_sem, recv_sem
 
@@ -709,8 +713,8 @@
         me = lax.axis_index("inner")
         peer = wrapped(me + step, self.inner)
         return remote(
-            self.src.at[peer],
-            self.dst.at[me],
+            self.src.at[:, peer] if self.second else self.src.at[peer],
+            self.dst.at[:, me] if self.second else self.dst.at[me],
             self.send_sem.at[step],
             self.recv_sem.at[step],
             lax.axis_index("outer"),
@@ -723,7 +727,11 @@
             self.copy(step).start()
 
         me = lax.axis_index("inner")
-        self.dst[me] = self.src[me]
+        if self.second:
+            for half in range(2):
+                self.dst[half, me] = self.src[half, me]
+        else:
+            self.dst[me] = self.src[me]
 
     def wait_recv(self):
         @pl.loop(1, self.inner)
@@ -740,145 +748,113 @@
     return jnp.where(value >= count, value - count, value)
 
 
-def owner_of(head, inner):
-    high = jnp.where(head >= inner, 1, 0)
-    return 2 * high, head - inner * high
-
-
 class ToOwner:
-    def __init__(self, inner, devices, src, dst, send_sem, recv_sem):
-        self.inner, self.devices, self.src, self.dst = inner, devices, src, dst
+    def __init__(self, count, src, dst, send_sem, recv_sem):
+        self.count, self.src, self.dst = count, src, dst
         self.send_sem, self.recv_sem = send_sem, recv_sem
-
-    def place(self):
-        return lax.axis_index("outer"), lax.axis_index("inner")
-
-    def copy(self, head):
-        outer, inner = self.place()
-        to_outer, to_inner = owner_of(head, self.inner)
-        me = outer * self.inner + inner
+        self.mine, self.place = lax.axis_index("outer"), lax.axis_index("inner")
+
+    def copy(self, half):
         return remote(
-            self.src.at[head],
-            self.dst.at[me],
-            self.send_sem.at[head],
-            self.recv_sem.at[me],
-            to_outer,
-            to_inner,
-        )
-
-    def each(self, other, own):
-        outer, inner = self.place()
-        me = outer * self.inner + inner
-
-        first = wrapped(me, HEADS)
-
-        @pl.loop(0, HEADS)
-        def _(step):
-            head = wrapped(step + first, HEADS)
-            to_outer, to_inner = owner_of(head, self.inner)
-            at_home = (to_outer * self.inner + to_inner) == me
-
-            @pl.when(jnp.logical_not(at_home))
+            self.src.at[half],
+            self.dst.at[self.mine],
+            self.send_sem.at[half],
+            self.recv_sem.at[self.mine],
+            2 * half,
+            self.place,
+        )
+
+    def start(self):
+        for half in range(2):
+
+            @pl.when(self.mine != 2 * half)
             def _():
-                other(head)
-
-            if own is not None:
-
-                @pl.when(at_home)
-                def _():
-                    own(head, me)
-
-    def start(self):
-        def keep(head, me):
-            self.dst[me] = self.src[head]
-
-        self.each(lambda head: self.copy(head).start(), keep)
+                self.copy(half).start()
+
+            @pl.when(self.mine == 2 * half)
+            def _():
+                self.dst[self.mine] = self.src[half]
 
     def wait_recv(self):
-        outer, inner = self.place()
-        me = outer * self.inner + inner
-
-        for source_outer in range(self.devices // self.inner):
-
-            @pl.loop(0, self.inner)
-            def _(source_inner):
-                source = source_outer * self.inner + source_inner
-
-                @pl.when(source != me)
-                def _():
-                    remote(
-                        self.src.at[0],
-                        self.dst.at[source],
-                        self.send_sem.at[0],
-                        self.recv_sem.at[source],
-                        source_outer,
-                        source_inner,
-                    ).wait_recv()
-
-    def wait_send(self):
-        self.each(lambda head: self.copy(head).wait_send(), None)
-
-
-def others(inner, devices, act):
-    mine, me = lax.axis_index("outer"), lax.axis_index("inner")
-    count = devices // inner
-    for step in range(count):
-        to_outer = wrapped(mine + step, count)
-
-        @pl.loop(1 if step == 0 else 0, inner)
-        def _(place):
-            act(to_outer, wrapped(me + place, inner))
-
-
-class FromOwner:
-    def __init__(self, inner, devices, src, dst, send_sem, recv_sem):
-        self.inner, self.devices, self.src, self.dst = inner, devices, src, dst
-        self.send_sem, self.recv_sem = send_sem, recv_sem
-
-    def copy(self, to_outer, to_inner):
-        target = to_outer * self.inner + to_inner
-        outer, inner = lax.axis_index("outer"), lax.axis_index("inner")
-        head = outer // 2 * self.inner + inner
-        return remote(
-            self.src.at[target],
-            self.dst.at[head],
-            self.send_sem.at[target],
-            self.recv_sem.at[head],
-            to_outer,
-            to_inner,
-        )
-
-    def start(self):
-        outer, inner = lax.axis_index("outer"), lax.axis_index("inner")
-        me = outer * self.inner + inner
-        others(self.inner, self.devices, lambda *place: self.copy(*place).start())
-        self.dst[outer // 2 * self.inner + inner] = self.src[me]
-
-    def wait_recv(self):
-        me = lax.axis_index("outer") * self.inner + lax.axis_index("inner")
-
-        @pl.loop(0, HEADS)
-        def _(head):
-            from_outer, from_inner = owner_of(head, self.inner)
-
-            @pl.when((from_outer * self.inner + from_inner) != me)
+        for source in range(self.count):
+
+            @pl.when(self.mine != source)
             def _():
                 remote(
                     self.src.at[0],
-                    self.dst.at[head],
+                    self.dst.at[source],
                     self.send_sem.at[0],
-                    self.recv_sem.at[head],
-                    from_outer,
-                    from_inner,
+                    self.recv_sem.at[source],
+                    source,
+                    self.place,
                 ).wait_recv()
 
     def wait_send(self):
-        others(self.inner, self.devices, lambda *place: self.copy(*place).wait_send())
+        for half in range(2):
+
+            @pl.when(self.mine != 2 * half)
+            def _():
+                self.copy(half).wait_send()
+
+
+class FromOwner:
+    def __init__(self, count, src, dst, send_sem, recv_sem):
+        self.count, self.src, self.dst = count, src, dst
+        self.send_sem, self.recv_sem = send_sem, recv_sem
+        self.mine, self.place = lax.axis_index("outer"), lax.axis_index("inner")
+
+    def copy(self, target):
+        half = self.mine // 2
+        return remote(
+            self.src.at[target],
+            self.dst.at[half],
+            self.send_sem.at[target],
+            self.recv_sem.at[half],
+            target,
+            self.place,
+        )
+
+    def each(self, act):
+        for target in range(self.count):
+
+            @pl.when(self.mine != target)
+            def _():
+                act(self.copy(target))
+
+    def start(self):
+        self.each(lambda copy: copy.start())
+        self.dst[self.mine // 2] = self.src[self.mine]
+
+    def wait_recv(self):
+        for half in range(2):
+
+            @pl.when(self.mine != 2 * half)
+            def _():
+                remote(
+                    self.src.at[0],
+                    self.dst.at[half],
+                    self.send_sem.at[0],
+                    self.recv_sem.at[half],
+                    2 * half,
+                    self.place,
+                ).wait_recv()
+
+    def wait_send(self):
+        self.each(lambda copy: copy.wait_send())
+
+
+def neighbours(inner, count, act):
+    mine, me = lax.axis_index("outer"), lax.axis_index("inner")
+    for step in range(1, count):
+        act(wrapped(mine + step, count), me)
+    for step in range(1, inner):
+        act(mine, wrapped(me + step, inner))
 
 
 def whole_kernel(inner, devices, len_ref, q_ref, k_ref, v_ref, c_ref, att_ref, dq_ref, dk_ref, dv_ref, *scratch):
     (xp, near_out, near_lse, plane_t, near_grads, acc) = scratch[:6]
-    staged, gcs, gcr, load_sem = scratch[26:]
+    staged, gcs, gcr, load_sem, m1, m2, m3, m4 = scratch[26:]
+    count = devices // inner
     (g1s, g1r, s1s, s1r, g2s, g2r, s2s, s2r, g3s, g3r, s3s, s3r, g4s, g4r, s4s, s4r) = scratch[6:22]
     group_send, group_recv, slide_send, slide_recv = scratch[22:26]
     outer, place = lax.axis_index("outer"), lax.axis_index("inner")
@@ -887,14 +863,16 @@
     def group_exchange(phase, src, dst):
         return Group(inner, src, dst, group_send.at[phase], group_recv.at[phase])
 
+    def slide_inner(phase, src, dst):
+        return Group(inner, src, dst, group_send.at[phase], group_recv.at[phase], True)
+
     def slide_exchange(kind, phase, src, dst):
-        return kind(inner, devices, src, dst, slide_send.at[phase], slide_recv.at[phase])
-
-    group1, slide1 = group_exchange(0, g1s, g1r), slide_exchange(ToOwner, 0, s1s, s1r)
-    group2, slide2 = group_exchange(1, g2s, g2r), slide_exchange(FromOwner, 1, s2s, s2r)
-    group3, slide3 = group_exchange(2, g3s, g3r), slide_exchange(ToOwner, 2, s3s, s3r)
-    group4, slide4 = group_exchange(3, g4s, g4r), slide_exchange(FromOwner, 3, s4s, s4r)
-
+        return kind(count, src, dst, slide_send.at[phase], slide_recv.at[phase])
+
+    group1, near1, slide1 = group_exchange(0, g1s, g1r), slide_inner(5, s1s, m1), slide_exchange(ToOwner, 0, m1, s1r)
+    group2, near2, slide2 = group_exchange(1, g2s, g2r), slide_inner(6, m2, s2r), slide_exchange(FromOwner, 1, s2s, m2)
+    group3, near3, slide3 = group_exchange(2, g3s, g3r), slide_inner(7, s3s, m3), slide_exchange(ToOwner, 2, m3, s3r)
+    group4, near4, slide4 = group_exchange(3, g4s, g4r), slide_inner(8, m4, s4r), slide_exchange(FromOwner, 3, s4s, m4)
     group_c = group_exchange(4, gcs, gcr)
     barrier = pltpu.get_barrier_semaphore()
 
@@ -907,13 +885,15 @@
     ]
     for load in loads:
         load.start()
-    others(inner, devices, greet)
+    neighbours(inner, count, greet)
     for load in loads:
         load.wait()
     prep_kernel(len_ref, *[staged.at[a] for a in range(4)], xp, g1s, gcs, s1s)
-    pl.semaphore_wait(barrier, devices - 1)
+    pl.semaphore_wait(barrier, inner + count - 2)
+    near1.start()
+    group1.start()
+    near1.wait_recv()
     slide1.start()
-    group1.start()
     group_c.start()
     near_fwd_kernel(len_ref, xp, near_out, near_lse)
 
@@ -926,11 +906,15 @@
     group1.wait_recv()
     group_fwd(g1r, g2s)
     group2.start()
+    slide2.wait_recv()
+    near2.start()
     group2.wait_recv()
-    slide2.wait_recv()
+    near2.wait_recv()
     combine_kernel(xp, near_out, near_lse, g2r, s2r, att_ref, plane_t, g3s, s3s, acc)
+    near3.start()
+    group3.start()
+    near3.wait_recv()
     slide3.start()
-    group3.start()
     near_bwd_kernel(len_ref, xp, plane_t, near_grads)
 
     @pl.when(is_owner)
@@ -943,10 +927,12 @@
     group3.wait_recv()
     group_bwd(g1r, gcr, g3r, g4s)
     group4.start()
+    slide4.wait_recv()
+    near4.start()
     group4.wait_recv()
-    slide4.wait_recv()
+    near4.wait_recv()
     final_kernel(near_grads, g4r, s4r, dq_ref, dk_ref, dv_ref, acc)
-    for sent in (group1, slide1, group_c, group2, group3, slide3, group4):
+    for sent in (near1, near2, near3, near4, group1, slide1, group_c, group2, group3, slide3, group4):
         sent.wait_send()
 
     @pl.when(is_owner)
@@ -971,13 +957,19 @@
         pltpu.VMEM((3, tiles, width), F32),
         pltpu.VMEM((3, tiles, width), F32),
     ]
-    scratch += both(inner, inner, (3, 32, LANES), BF) + both(HEADS, devices, (16, LANES), BF)
-    scratch += both(inner, inner, (32, LANES), BF) + both(devices, HEADS, (8, LANES), BF)
-    scratch += both(inner, inner, (8, LANES), F32) + both(HEADS, devices, (8, LANES), F32)
-    scratch += both(inner, inner, (3, 32, LANES), BF) + both(devices, HEADS, (16, LANES), BF)
-    scratch += [pltpu.SemaphoreType.DMA((5, inner))] * 2 + [pltpu.SemaphoreType.DMA((4, devices))] * 2
+    scratch += both(inner, inner, (3, 32, LANES), BF) + both(2, devices // inner, (inner, 16, LANES), BF)
+    scratch += both(inner, inner, (32, LANES), BF) + both(devices // inner, 2, (inner, 8, LANES), BF)
+    scratch += both(inner, inner, (8, LANES), F32) + both(2, devices // inner, (inner, 8, LANES), F32)
+    scratch += both(inner, inner, (3, 32, LANES), BF) + both(devices // inner, 2, (inner, 16, LANES), BF)
+    scratch += [pltpu.SemaphoreType.DMA((9, inner))] * 2 + [pltpu.SemaphoreType.DMA((4, devices // inner))] * 2
     scratch += [pltpu.VMEM((4, tiles, width), BF)] + both(inner, inner, (32, LANES), BF)
     scratch += [pltpu.SemaphoreType.DMA((4,))]
+    scratch += [
+        pltpu.VMEM((2, inner, 16, LANES), BF),
+        pltpu.VMEM((2, inner, 8, LANES), BF),
+        pltpu.VMEM((2, inner, 8, LANES), F32),
+        pltpu.VMEM((2, inner, 16, LANES), BF),
+    ]
     return tuple(
         pl.pallas_call(
             lambda *refs: whole_kernel(inner, devices, *refs),
@@ -986,7 +978,7 @@
             out_specs=[vmem] * 4,
             scratch_shapes=scratch,
             compiler_params=pltpu.CompilerParams(
-                collective_id=0, has_side_effects=True, vmem_limit_bytes=48 * 1024 * 1024
+                collective_id=0, has_side_effects=True, vmem_limit_bytes=60 * 1024 * 1024
             ),
         )(row_lengths, *tiles_in)
     )

time: 47.9 us -> 48.1 us (level)
  Pallas kernels: 39.9 us -> 42.9 us
  local copies, waits for them, and re-layouts: 7.06 us -> 4.33 us
    pallas_call x1, Pallas kernels: 39.9 us -> 42.9 us  [fast_local(): pl.pallas_call(lambda *refs: whole_kernel(inner, devices, *refs), out_sha...]
    unnamed x14 -> x10, local copies, waits for them, and re-layouts: 7.06 us -> 4.33 us
where the time goes in v4:
time: 48.1 us; the launch traced here: 47.8 us
  Pallas kernels  42.9 us (89%)
  local copies, waits for them, and re-layouts  4.33 us (9%)
  between operations  0.65 us (1%)
    pallas_call x1, Pallas kernels, fast_local(): pl.pallas_call(lambda *refs: whole_kernel(inner, devices, *refs), out_sha...  42.9 us
    unnamed x10, local copies, waits for them, and re-layouts  4.33 us

profile of v4, /device:TPU:0, one launch (start us, length us, event | category | flops | bytes accessed | tf_op | source)
XLA Modules:
  0.0 47.8 jit_solution(1809001885422419423)
XLA Ops:
  0.6 42.9 %shard_map.84 = (bf16[128,768]{1,0:T(8,128)(2,1)}, bf16[128,768]{1,0:T(8,128)(2,1)}, bf16[128,768]{1,0:T(8,128)(2,1)}, bf16[128,768]{1,0:T(8,128)(2,1)}) custom-call(s32[4]{0:T(128)} %refs_0_.1, bf16[128,768]{1,0:T(8,128)(2,1)} %refs_1_.1, bf16[128,768]{1,0:T(8,128)(2,1)} %refs_2_.1, bf16[128,768]{1,0:T(8,128)(2,1)} %refs_3_.1, bf16[128,768]{1,0:T(8,128)(2,1)} %refs_4_.1), custom_call_target="tpu_custom_call" | custom-call | tf_op jit(solution)/shard_map/pallas_call | solution.py:974
  43.5 0.0 copy-start.2
  43.5 1.7 %copy.13 = bf16[128,768]{1,0:T(8,128)(2,1)} copy(bf16[128,768]{1,0:T(8,128)(2,1)} %get-tuple-element.8) | data formatting | bytes 393216
  45.2 0.0 copy-done.2
  45.2 0.0 copy-start.1
  45.2 0.7 %copy.14 = bf16[128,768]{1,0:T(8,128)(2,1)} copy(bf16[128,768]{1,0:T(8,128)(2,1)S(1)} %copy-done.2) | data formatting | bytes 393216
  45.8 0.3 copy-done.1
  46.2 0.0 copy-start
  46.2 0.7 %copy.15 = bf16[128,768]{1,0:T(8,128)(2,1)} copy(bf16[128,768]{1,0:T(8,128)(2,1)S(1)} %copy-done.1) | data formatting | bytes 393216
  46.8 0.3 copy-done
  47.2 0.7 %copy.16 = bf16[128,768]{1,0:T(8,128)(2,1)} copy(bf16[128,768]{1,0:T(8,128)(2,1)S(1)} %copy-done) | data formatting | bytes 393216
Async XLA Ops:
  43.5 1.7 %copy-start.2 = (bf16[128,768]{1,0:T(8,128)(2,1)S(1)}, bf16[128,768]{1,0:T(8,128)(2,1)}, u32[]{:S(2)}) copy-start(bf16[128,768]{1,0:T(8,128)(2,1)} %get-tuple-element.9) | copy-start | bytes 589828
  45.2 1.0 %copy-start.1 = (bf16[128,768]{1,0:T(8,128)(2,1)S(1)}, bf16[128,768]{1,0:T(8,128)(2,1)}, u32[]{:S(2)}) copy-start(bf16[128,768]{1,0:T(8,128)(2,1)} %get-tuple-element.10) | copy-start | bytes 589828
  46.2 1.0 %copy-start = (bf16[128,768]{1,0:T(8,128)(2,1)S(1)}, bf16[128,768]{1,0:T(8,128)(2,1)}, u32[]{:S(2)}) copy-start(bf16[128,768]{1,0:T(8,128)(2,1)} %get-tuple-element.11) | copy-start | bytes 589828

commit v5 on v4

--- a/solution.py
+++ b/solution.py
@@ -978,7 +978,7 @@
             out_specs=[vmem] * 4,
             scratch_shapes=scratch,
             compiler_params=pltpu.CompilerParams(
-                collective_id=0, has_side_effects=True, vmem_limit_bytes=60 * 1024 * 1024
+                collective_id=0, has_side_effects=True, vmem_limit_bytes=64 * 1024 * 1024
             ),
         )(row_lengths, *tiles_in)
     )

time: 48.1 us -> 48.1 us (level)
  no operation moved by 1% of the time
where the time goes in v5:
time: 48.1 us; the launch traced here: 47.8 us
  Pallas kernels  42.9 us (89%)
  local copies, waits for them, and re-layouts  4.33 us (9%)
  between operations  0.65 us (1%)
    pallas_call x1, Pallas kernels, fast_local(): pl.pallas_call(lambda *refs: whole_kernel(inner, devices, *refs), out_sha...  42.9 us
    unnamed x10, local copies, waits for them, and re-layouts  4.33 us

profile of v5, /device:TPU:0, one launch (start us, length us, event | category | flops | bytes accessed | tf_op | source)
XLA Modules:
  0.0 47.8 jit_solution(1809001885422419423)
XLA Ops:
  0.6 42.9 %shard_map.84 = (bf16[128,768]{1,0:T(8,128)(2,1)}, bf16[128,768]{1,0:T(8,128)(2,1)}, bf16[128,768]{1,0:T(8,128)(2,1)}, bf16[128,768]{1,0:T(8,128)(2,1)}) custom-call(s32[4]{0:T(128)} %refs_0_.1, bf16[128,768]{1,0:T(8,128)(2,1)} %refs_1_.1, bf16[128,768]{1,0:T(8,128)(2,1)} %refs_2_.1, bf16[128,768]{1,0:T(8,128)(2,1)} %refs_3_.1, bf16[128,768]{1,0:T(8,128)(2,1)} %refs_4_.1), custom_call_target="tpu_custom_call" | custom-call | tf_op jit(solution)/shard_map/pallas_call | solution.py:974
  43.5 0.0 copy-start.2
  43.5 1.7 %copy.13 = bf16[128,768]{1,0:T(8,128)(2,1)} copy(bf16[128,768]{1,0:T(8,128)(2,1)} %get-tuple-element.8) | data formatting | bytes 393216
  45.2 0.0 copy-done.2
  45.2 0.0 copy-start.1
  45.2 0.7 %copy.14 = bf16[128,768]{1,0:T(8,128)(2,1)} copy(bf16[128,768]{1,0:T(8,128)(2,1)S(1)} %copy-done.2) | data formatting | bytes 393216
  45.8 0.3 copy-done.1
  46.2 0.0 copy-start
  46.2 0.7 %copy.15 = bf16[128,768]{1,0:T(8,128)(2,1)} copy(bf16[128,768]{1,0:T(8,128)(2,1)S(1)} %copy-done.1) | data formatting | bytes 393216
  46.8 0.3 copy-done
  47.2 0.7 %copy.16 = bf16[128,768]{1,0:T(8,128)(2,1)} copy(bf16[128,768]{1,0:T(8,128)(2,1)S(1)} %copy-done) | data formatting | bytes 393216
Async XLA Ops:
  43.5 1.7 %copy-start.2 = (bf16[128,768]{1,0:T(8,128)(2,1)S(1)}, bf16[128,768]{1,0:T(8,128)(2,1)}, u32[]{:S(2)}) copy-start(bf16[128,768]{1,0:T(8,128)(2,1)} %get-tuple-element.9) | copy-start | bytes 589828
  45.2 1.0 %copy-start.1 = (bf16[128,768]{1,0:T(8,128)(2,1)S(1)}, bf16[128,768]{1,0:T(8,128)(2,1)}, u32[]{:S(2)}) copy-start(bf16[128,768]{1,0:T(8,128)(2,1)} %get-tuple-element.10) | copy-start | bytes 589828
  46.2 1.0 %copy-start = (bf16[128,768]{1,0:T(8,128)(2,1)S(1)}, bf16[128,768]{1,0:T(8,128)(2,1)}, u32[]{:S(2)}) copy-start(bf16[128,768]{1,0:T(8,128)(2,1)} %get-tuple-element.11) | copy-start | bytes 589828
